TPU v7x, 128 devices: a whole 4x4x4 slice. The times are simulated.
128 devices in a mesh: seq: 32 (over z, x, core), mp: 4 (over y).
Axes of the slice: x: 4, y: 4, z: 4, core: 2. Of those that a mesh axis runs over, the one named last changes fastest.
Arguments:
- grad_rows: bfloat16 [16384, 8192], P('seq', 'mp'), may hold values from -6 to 6
- img_start: int32 [256], replicated, may hold values from 0 to 16380, as said below
- img_len: int32 [256], replicated, may hold values from 4 to 64, as said below
- img_owner: int32 [256], replicated, may hold values from 0 to 31, as said below
- pre_act: bfloat16 [16384, 5120], P('seq', 'mp'), may hold values from -6 to 6
- w_out: bfloat16 [5120, 8192], P(None, 'mp'), may hold values from -0.0625 to 0.0625
Outputs:
- pre_grad: bfloat16 [16384, 5120], P('seq', 'mp')
- weight_grad: bfloat16 [5120, 8192], P('seq', 'mp')
Inputs may be any that keep to these rules, and one draw needn't show every extreme that they name: Image i lies inside positions i * 64 to (i + 1) * 64 - 1: img_start[i] - i * 64 + img_len[i] <= 64. `img_len`: A multiple of 4. In every draw some owner has all its images of exactly 64 merged tokens. `img_owner`: the images i with one value of i % 8 all have different owners, and so do the 8 images of one stripe (images i with one value of i // 8).
All inputs are finite; a program needn't handle non-finite values.
Results may differ from a plain program's by a relative error of at most 0.02.
Values may be sent and summed in bfloat16 or wider, within the bound.
No kernel may reach another device: no remote copies, remote signals or barrier semaphores. Data moves between devices by JAX's collectives and lax.ppermute only.
A program may use at most 192 MiB of HBM per device.

v0:
```python
import math

import jax
import jax.numpy as jnp
from jax import lax
from jax.sharding import PartitionSpec as P

FRAME = 64


def split_up(value, dim, peers):
    dims = value.shape
    pieces = value.reshape(*dims[:dim], peers, dims[dim] // peers, *dims[dim + 1 :])
    return jnp.moveaxis(pieces, dim, 0)


def sum_at_owner(value, axis, dim):
    pieces = split_up(value, dim, lax.axis_size(axis))
    arrived = lax.all_to_all(pieces, axis, split_axis=0, concat_axis=0, tiled=True)
    return arrived.astype(jnp.float32).sum(axis=0)


def gelu_parts(values):
    normal_cdf = 0.5 * (1.0 + lax.erf(values * 0.7071067811865476))
    density = jnp.exp(-0.5 * values * values) * 0.3989422804014327
    return (values * normal_cdf, normal_cdf + values * density)


def local(grad_rows, img_start, img_len, img_owner, pre_act, w_out):
    stripe = grad_rows.shape[0]
    quarter = grad_rows.shape[1]
    frames = stripe // FRAME
    owners_total = lax.axis_size("seq")
    here = lax.axis_index("seq")
    within = jnp.arange(FRAME, dtype=jnp.int32)
    first_image = here * frames
    starts = lax.dynamic_slice_in_dim(img_start, first_image, frames)
    lengths = lax.dynamic_slice_in_dim(img_len, first_image, frames)
    my_owners = lax.dynamic_slice_in_dim(img_owner, first_image, frames)
    offsets = starts - here * stripe
    row_ids = jnp.clip(offsets[:, None] + within[None, :], 0, stripe - 1)
    filled = within[None, :] < lengths[:, None]
    blocks = jnp.where(filled[:, :, None], grad_rows[row_ids], jnp.zeros((), jnp.bfloat16))
    owner_ids = jnp.arange(owners_total, dtype=jnp.int32)
    placing = (my_owners[None, :] == owner_ids[:, None]).astype(jnp.bfloat16)
    outgoing = jnp.dot(
        placing, blocks.reshape(frames, FRAME * quarter), preferred_element_type=jnp.float32
    )
    outgoing = outgoing.astype(jnp.bfloat16).reshape(owners_total * FRAME, quarter)
    received = lax.all_to_all(outgoing, "seq", split_axis=0, concat_axis=0, tiled=True)
    choosing = (img_owner.reshape(owners_total, frames) == here).T.astype(jnp.bfloat16)
    routed = jnp.dot(
        choosing,
        received.reshape(owners_total, FRAME * quarter),
        preferred_element_type=jnp.float32,
    )
    routed = routed.astype(jnp.bfloat16).reshape(stripe, quarter)
    hidden_terms = lax.dot_general(
        routed, w_out, (((1,), (1,)), ((), ())), preferred_element_type=jnp.float32
    )
    hidden_grad = sum_at_owner(hidden_terms.astype(jnp.bfloat16), "mp", 1)
    _, derivative = gelu_parts(pre_act.astype(jnp.float32))
    pre_grad = (hidden_grad * derivative).astype(jnp.bfloat16)
    pre_full = lax.all_gather(pre_act, "mp", axis=1, tiled=True)
    activation, _ = gelu_parts(pre_full.astype(jnp.float32))
    activation = activation.astype(jnp.bfloat16)
    factor = 1.0 / math.sqrt(owners_total * stripe)
    product = lax.dot_general(
        activation, routed, (((0,), (0,)), ((), ())), preferred_element_type=jnp.float32
    )
    weight_grad = lax.psum_scatter(
        (product * factor).astype(jnp.bfloat16), "seq", scatter_dimension=0, tiled=True
    )
    return (pre_grad, weight_grad)


def solution(mesh):
    return jax.shard_map(
        local,
        mesh=mesh,
        in_specs=(P("seq", "mp"), P(), P(), P(), P("seq", "mp"), P(None, "mp")),
        out_specs=(P("seq", "mp"), P("seq", "mp")),
        check_vma=False,
    )
```

profile of v0, /device:TPU:8, one launch (start us, length us, event | category | flops | bytes accessed | tf_op | source)
XLA Modules:
  0.0 315.4 jit_solution(6018020969842371670)
XLA Ops:
  7.2 0.9 dynamic-slice_subtract_fusion
  8.3 0.8 dynamic_slice.10
  9.1 3.3 %gather_fusion = bf16[512,2048]{1,0:T(8,128)(2,1)} fusion(bf16[512,2048]{1,0:T(8,128)(2,1)S(1)} %copy-done, s32[1024]{0:T(1024)S(1)} %pad_clamp_fusion), kind=kCustom, calls=%fused_computation | custom fusion | bytes 4196352 | tf_op jit(solution)/shard_map/gather | solution.py:43
  12.4 1.8 select_bitcast_fusion
  14.2 1.2 copy.10
  15.5 5.5 %convolution_convert_fusion = bf16[32,131072]{1,0:T(8,128)(2,1)} fusion(bf16[8,131072]{1,0:T(8,128)(2,1)S(1)} %bitcast.28, s32[8]{0:T(128)S(1)} %dynamic_slice.9), kind=kOutput, calls=%fused_computation.1 | convolution fusion | flops 71303424 | bytes 10485792 | tf_op jit(solution)/shard_map/dot_general | solution.py:46
  21.0 11.4 %copy.11 = bf16[4,8,64,2048]{3,2,1,0:T(8,128)(2,1)} copy(bf16[4,8,64,2048]{3,1,2,0:T(8,128)(2,1)} %bitcast.25) | data formatting | bytes 16777216
  32.4 8.3 %all-to-all-start = ((bf16[32,64,2048]{2,1,0:T(8,128)(2,1)}), bf16[32,64,2048]{2,1,0:T(8,128)(2,1)}, u32[]{:S(2)}, u32[]{:S(2)}) async-start(bf16[32,64,2048]{2,1,0:T(8,128)(2,1)} %bitcast.24), calls=%async_computation | async-start | bytes 16777216 | tf_op jit(solution)/shard_map/all_to_all | solution.py:50
  40.8 0.7 all-gather.2.cloned.1.call-update
  41.4 0.2 reduce-scatter.2.cloned.1.call-start
  41.7 0.1 eq.24
  41.8 104.8 %all-to-all-done = bf16[32,64,2048]{2,1,0:T(8,128)(2,1)} async-done(((bf16[32,64,2048]{2,1,0:T(8,128)(2,1)}), bf16[32,64,2048]{2,1,0:T(8,128)(2,1)}, u32[]{:S(2)}, u32[]{:S(2)}) %all-to-all-start) | async-done | bytes 8388640 | tf_op jit(solution)/shard_map/all_to_all | solution.py:50
  146.6 11.4 %copy.12 = bf16[4,8,64,2048]{3,1,2,0:T(8,128)(2,1)} copy(bf16[4,8,64,2048]{3,2,1,0:T(8,128)(2,1)} %bitcast.9) | data formatting | bytes 16777216
  157.9 4.6 %convolution_convert_fusion.1 = bf16[8,131072]{1,0:T(8,128)(2,1)S(1)} fusion(pred[32,8]{1,0:T(32,128)(4,1)S(1)} %eq.24, bf16[32,131072]{1,0:T(8,128)(2,1)} %bitcast.23), kind=kOutput, calls=%fused_computation.2 | convolution fusion | flops 68157440 | bytes 10486016 | tf_op jit(solution)/shard_map/dot_general | solution.py:52
  162.6 2.3 reshape.91
  164.9 18.5 %multiply_convert_fusion = bf16[5120,2048]{1,0:T(8,128)(2,1)} fusion(bf16[512,2048]{1,0:T(8,128)(2,1)} %reshape.91, bf16[512,5120]{1,0:T(8,128)(2,1)} %all-gather.2.cloned.1.call-done), kind=kOutput, calls=%fused_computation.3 | convolution fusion | flops 10774118400 | bytes 28311552 | tf_op jit(solution)/shard_map/dot_general | solution.py:68
  183.4 1.6 copy-done.3
  184.9 17.1 %convolution_convert_fusion.2 = bf16[512,5120]{1,0:T(8,128)(2,1)} fusion(bf16[512,2048]{1,0:T(8,128)(2,1)S(1)} %copy-done.3, bf16[5120,2048]{1,0:T(8,128)(2,1)} %param.11), kind=kOutput, calls=%fused_computation.11 | convolution fusion | flops 10740039680 | bytes 28311552 | tf_op jit(solution)/shard_map/dot_general | solution.py:58
  202.0 3.4 %copy.14 = bf16[64,4,8,1280]{3,2,0,1:T(8,128)(2,1)S(1)} copy(bf16[64,4,8,1280]{3,2,1,0:T(8,128)(2,1)} %bitcast.29) | data formatting | bytes 10485760 | tf_op jit(solution)/shard_map/reshape | solution.py:13
  205.4 57.2 %all_to_all.14 = bf16[4,512,1280]{2,1,0:T(8,128)(2,1)S(1)} all-to-all(bf16[4,512,1280]{2,1,0:T(8,128)(2,1)S(1)} %bitcast.26), channel_id=1, replica_groups=mesh['seq'=32,'mp'=4] {'mp'}, dimensions={0} | all-to-all | bytes 10485760 | tf_op jit(solution)/shard_map/all_to_all | solution.py:19
  262.6 0.7 convert_reduce_fusion
  263.3 0.9 copy-done.2
  264.1 2.0 fusion.15
  266.1 42.4 %reduce-scatter.2.cloned.1.call-done = bf16[160,2048]{1,0:T(8,128)(2,1)} async-done(((bf16[5120,2048]{1,0:T(8,128)(2,1)}), bf16[160,2048]{1,0:T(8,128)(2,1)}) %reduce-scatter.2.cloned.1.call-update) | async-done | bytes 655376 | tf_op jit(solution)/shard_map/reduce_scatter | solution.py:71
  (17 shorter events, 0.4 us)
Async XLA Ops:
  7.2 1.9 copy-start
  14.2 1.2 copy-start.4
  32.4 114.2 %all-to-all-start = ((bf16[32,64,2048]{2,1,0:T(8,128)(2,1)}), bf16[32,64,2048]{2,1,0:T(8,128)(2,1)}, u32[]{:S(2)}, u32[]{:S(2)}) async-start(bf16[32,64,2048]{2,1,0:T(8,128)(2,1)} %bitcast.24), calls=%async_computation | async-start | bytes 16777216 | tf_op jit(solution)/shard_map/all_to_all | solution.py:50
  40.7 124.2 %all-gather.2.cloned.1.call-start = ((), (), s32[]{:S(2)}) async-start(), calls=%async_computation.3 | async-start | bytes 6553600 | tf_op jit(solution)/shard_map/all_gather | solution.py:64
  41.4 267.1 %reduce-scatter.2.cloned.1.call-start = ((), (), s32[]{:S(2)}) async-start(), calls=%async_computation.4 | async-start | bytes 21626880 | tf_op jit(solution)/shard_map/reduce_scatter | solution.py:71
  183.3 1.6 copy-start.3
  262.6 1.6 copy-start.2
  262.6 46.0 %copy-start.1 = (bf16[512,2048]{1,0:T(8,128)(2,1)S(1)}, bf16[512,2048]{1,0:T(8,128)(2,1)}, u32[]{:S(2)}) copy-start(bf16[512,2048]{1,0:T(8,128)(2,1)} %param.6) | copy-start | bytes 6291460
Sparse Core Ops, SparseCore 0:
  43.2 57.9 all-gather.1
  183.5 125.0 reduce-scatter.1
where the time goes:
time: 316 us; the launch traced here: 315 us
  waiting for transfers between devices  148 us (47%)
  blocking collectives  57.2 us (18%)
  matrix products  45.7 us (14%)
  local copies, waits for them, and re-layouts  36.4 us (12%)
  between operations  14.1 us (4%)
  starting transfers between devices  8.55 us (3%)
  other arithmetic  5.57 us (2%)
    all_to_all x1, waiting for transfers between devices, local(): lax.all_to_all(outgoing, 'seq', split_axis=0, concat_axis=0, tiled=True)  105 us
    all_to_all x1, blocking collectives, sum_at_owner(): lax.all_to_all(pieces, axis, split_axis=0, concat_axis=0, tiled=True)  57.2 us
    reduce_scatter x1, waiting for transfers between devices, local(): lax.psum_scatter((product * factor).astype(jnp.bfloat16), 'seq', scatter_...  42.4 us
    unnamed x13, local copies, waits for them, and re-layouts  26.3 us
    dot_general x1, matrix products, local(): lax.dot_general(activation, routed, (((0,), (0,)), ((), ())), preferred_e...  18.5 us
    dot_general x1, matrix products, local(): lax.dot_general(routed, w_out, (((1,), (1,)), ((), ())), preferred_elemen...  17.1 us
    all_to_all x1, starting transfers between devices, local(): lax.all_to_all(outgoing, 'seq', split_axis=0, concat_axis=0, tiled=True)  8.29 us
  transfers between devices with their start and end apart: 3, of which 2 were waited for; matrix products, arithmetic and copies ran while one was open for 13% of the time, Pallas kernels for 0%

commit v1 on v0

v1 whole, which is shorter than its diff:
```python
import math

import jax
import jax.numpy as jnp
from jax import lax
from jax.experimental import pallas as pl
from jax.experimental.pallas import tpu as pltpu
from jax.sharding import Mesh
from jax.sharding import PartitionSpec as P

FRAME = 64
SEQ = ("z", "x", "core")


def flip(value, axis, mask):
    size = lax.axis_size(axis)
    return lax.ppermute(value, axis, [(i, i ^ mask) for i in range(size)])


def gelu_parts(values):
    normal_cdf = 0.5 * (1.0 + lax.erf(values * 0.7071067811865476))
    density = jnp.exp(-0.5 * values * values) * 0.3989422804014327
    return (values * normal_cdf, normal_cdf + values * density)


def place_kernel(owner_ref, blocks_ref, out_ref, staged, sem):
    def move(i, carry):
        staged[owner_ref[i]] = blocks_ref[i]
        return carry

    lax.fori_loop(0, blocks_ref.shape[0], move, 0)
    copy = pltpu.make_async_copy(staged, out_ref, sem)
    copy.start()
    copy.wait()


def place(owner, blocks):
    return pl.pallas_call(
        place_kernel,
        out_shape=jax.ShapeDtypeStruct(blocks.shape, blocks.dtype),
        in_specs=[pl.BlockSpec(memory_space=pltpu.SMEM), pl.BlockSpec(memory_space=pltpu.VMEM)],
        out_specs=pl.BlockSpec(memory_space=pltpu.HBM),
        scratch_shapes=[pltpu.VMEM(blocks.shape, blocks.dtype), pltpu.SemaphoreType.DMA],
        compiler_params=pltpu.CompilerParams(vmem_limit_bytes=12 << 20),
        cost_estimate=pl.CostEstimate(
            flops=0, transcendentals=0, bytes_accessed=2 * blocks.size * blocks.dtype.itemsize
        ),
    )(owner, blocks)


def hidden_kernel(rows_ref, weights_ref, out_ref):
    terms = dot(rows_ref[...], weights_ref[...], ((1,), (1,)))
    out_ref[0] = terms.astype(out_ref.dtype)


def hidden_terms(rows, weights, first, count, width):
    tokens, depth = rows.shape
    per_device = weights.shape[0] // 4 // width
    return pl.pallas_call(
        hidden_kernel,
        grid=(4, count),
        out_shape=jax.ShapeDtypeStruct((4, tokens, count * width), jnp.bfloat16),
        in_specs=[
            pl.BlockSpec((tokens, depth), lambda d, j: (0, 0)),
            pl.BlockSpec((width, depth), lambda d, j: (d * per_device + first + j, 0)),
        ],
        out_specs=pl.BlockSpec((1, tokens, width), lambda d, j: (d, 0, j)),
        compiler_params=pltpu.CompilerParams(vmem_limit_bytes=16 << 20),
        cost_estimate=pl.CostEstimate(
            flops=8 * tokens * depth * count * width,
            transcendentals=0,
            bytes_accessed=2 * (tokens * depth + 4 * count * width * (depth + tokens)),
        ),
    )(rows, pltpu.with_memory_space_constraint(weights, pltpu.HBM))


def dot(lhs, rhs, dims):
    return lax.dot_general(lhs, rhs, (dims, ((), ())), preferred_element_type=jnp.float32)


def wide(value):
    return value.astype(jnp.float32)


def narrow(value):
    return value.astype(jnp.bfloat16)


def take(value, masks, axis):
    parts = [lax.dynamic_slice_in_dim(value, m, 1, axis) for m in masks]
    return jnp.concatenate(parts, axis)


def after(value, *others):
    return lax.optimization_barrier((value, *others))[0]


def gather_ring(value, gate):
    half = value.shape[0] // 2
    one, three = after((flip(value, "y", 1), flip(value, "y", 3)), gate)
    two = jnp.concatenate([flip(one[:half], "y", 3), flip(three[half:], "y", 1)], axis=0)
    return jnp.stack([value, one, two, three])


def product(part, rhs):
    return narrow(dot(part, rhs, ((1,), (0,)))).reshape(2, 4, -1, rhs.shape[1])


SENT = {1: slice(1, 3), 3: slice(2, 4)}
HELD = {1: slice(3, 5), 3: slice(0, 2)}
OWN, FAR = {1: 1, 3: 0}, {1: 0, 3: 1}
OWN_SENT, FAR_SENT = {1: 0, 3: 1}, {1: 1, 3: 0}


def scatter_first(arrived, kept, axis, near):
    far = 4 - near
    arrived_far = flip(narrow(wide(kept[FAR[near]]) + wide(arrived[FAR_SENT[near]])), axis, far)
    return narrow(wide(kept[OWN[near]]) + wide(arrived[OWN_SENT[near]]) + wide(arrived_far))


def scatter_second(total, axis, near):
    far = 4 - near
    arrived = flip(total[SENT[near]], axis, near)
    arrived_far = flip(narrow(wide(total[far]) + wide(arrived[FAR_SENT[near]])), axis, far)
    return wide(total[0]) + wide(arrived[OWN_SENT[near]]) + wide(arrived_far)


def local(grad_rows, img_start, img_len, img_owner, pre_act, w_out):
    stripe, quarter = grad_rows.shape
    owners_total = lax.axis_size(SEQ)
    frames = stripe // FRAME
    here = lax.axis_index(SEQ)
    x, y, z, core = (lax.axis_index(a) for a in ("x", "y", "z", "core"))
    piece = stripe // owners_total

    spread = lax.all_to_all(
        grad_rows.reshape(owners_total, piece, quarter), SEQ, split_axis=0, concat_axis=0, tiled=True
    )
    owners = img_owner.reshape(owners_total, frames)
    frame_here = here * piece // FRAME
    owner_here = lax.dynamic_index_in_dim(owners, frame_here, 1, keepdims=False)
    placed = place(owner_here, spread)
    rows = lax.all_to_all(placed, SEQ, split_axis=0, concat_axis=0, tiled=True).reshape(stripe, quarter)

    mine = (owners == here).astype(jnp.int32)
    image_ids = jnp.arange(owners_total * frames, dtype=jnp.int32)
    offsets = (mine * (img_start - image_ids * FRAME).reshape(owners_total, frames)).sum(axis=0)
    lengths = (mine * img_len.reshape(owners_total, frames)).sum(axis=0)
    within = jnp.arange(FRAME, dtype=jnp.int32)
    target = jnp.arange(frames, dtype=jnp.int32)[:, None] * FRAME + offsets[:, None] + within[None, :]
    target = jnp.where(within[None, :] < lengths[:, None], target, -1).reshape(1, stripe)
    chosen = (target == jnp.arange(stripe, dtype=jnp.int32)[:, None]).astype(jnp.bfloat16)

    units = pre_act.shape[1]
    _, derivative = gelu_parts(dot(chosen, pre_act, ((1,), (0,))))
    activation, _ = gelu_parts(dot(pre_act, chosen, ((0,), (1,))))
    halves = take(narrow(activation).reshape(4, 2, units // 8, stripe), [x ^ m for m in range(4)], 0)
    own_half = lax.dynamic_index_in_dim(halves, core, 1, keepdims=False)
    other_half = flip(lax.dynamic_index_in_dim(halves, 1 - core, 1, keepdims=False), "core", 1)
    both = jnp.concatenate([own_half, other_half], axis=2)
    by_z = take(gather_ring(both, placed), [y ^ z ^ m for m in (0, 1, 2, 3, 0)], 0)
    by_x = jnp.swapaxes(by_z[:4], 0, 1)
    by_x = jnp.concatenate([by_x, by_x[:1]], axis=0)
    source = {"x": by_x, "z": by_z}

    lhs = {}
    for axis, near in (("x", 1), ("z", 1), ("x", 3), ("z", 3)):
        depth = 2 * stripe
        lhs[axis, near] = [source[axis][part[near]].reshape(-1, depth) for part in (SENT, HELD)]
    rows, weights, lhs = lax.optimization_barrier((rows, w_out, lhs))

    width = units // 5

    def hidden_rest(terms, gate, start, stop):
        arrived = after(lax.all_to_all(terms, "y", split_axis=0, concat_axis=0, tiled=True), gate)
        grad = narrow(wide(arrived).sum(axis=0) * derivative[:, start:stop])
        return narrow(dot(chosen, grad, ((0,), (0,))))

    early = hidden_terms(rows, weights, 0, 1, width)

    pair = jnp.concatenate([rows, flip(rows, "core", 1)], axis=0)
    span = quarter // 4
    plans = (("x", "z", 1), ("z", "x", 1), ("x", "z", 3), ("z", "x", 3))
    columns = [pair[:, i * span : (i + 1) * span] for i in range(4)]
    terms = [product(lhs[first, near][0], c) for (first, _, near), c in zip(plans, columns)]
    landed = [flip(term, first, near) for (first, _, near), term in zip(plans, terms)]

    late = hidden_terms(rows, after(weights, *terms), 1, 4, width)
    lhs = after(lhs, late)
    kept = [product(lhs[first, near][1], c) for (first, _, near), c in zip(plans, columns)]

    totals = [scatter_first(a, k, first, near) for a, k, (first, _, near) in zip(landed, kept, plans)]
    sums = [scatter_second(t, second, near) for t, (_, second, near) in zip(totals, plans)]
    factor = 1.0 / math.sqrt(owners_total * stripe)
    weight_grad = narrow(jnp.concatenate(sums, axis=1) * factor)
    parts = [hidden_rest(early, kept[0], 0, width), hidden_rest(late, kept[0], width, units)]
    pre_grad = jnp.concatenate(parts, axis=1)
    return (pre_grad, weight_grad)


def solution(mesh):
    grid = Mesh(mesh.devices.reshape(4, 4, 2, 4), ("z", "x", "core", "y"))
    return jax.shard_map(
        local,
        mesh=grid,
        in_specs=(P(SEQ, "y"), P(), P(), P(), P(SEQ, "y"), P(None, "y")),
        out_specs=(P(SEQ, "y"), P(SEQ, "y")),
        check_vma=False,
    )
```

time: 316 us -> 216 us (0.68)
  waiting for transfers between devices: 148 us -> 58.1 us
  blocking collectives: 57.2 us -> 0 us
  starting transfers between devices: 8.55 us -> 48.4 us
  other arithmetic: 5.57 us -> 33.1 us
  Pallas kernels: 0 us -> 23.9 us
  matrix products: 45.7 us -> 25.3 us
  between operations: 14.1 us -> 1.15 us
  local copies, waits for them, and re-layouts: 36.4 us -> 24.3 us
    all_to_all x1 -> x4, waiting for transfers between devices: 105 us -> 30.2 us  [the longest x1 25.1 us: local(): lax.all_to_all(grad_rows.reshape(owners_total, piece, quarter), SEQ, spli...]
    all_to_all x1 -> x0, blocking collectives: 57.2 us -> none  [sum_at_owner(): lax.all_to_all(pieces, axis, split_axis=0, concat_axis=0, tiled=True)]
    reduce_scatter x1 -> x0, waiting for transfers between devices: 42.4 us -> none  [local(): lax.psum_scatter((product * factor).astype(jnp.bfloat16), 'seq', scatter_...]
    ppermute x0 -> x22, waiting for transfers between devices: none -> 27.9 us  [flip(): return lax.ppermute(value, axis, [(i, i ^ mask) for i in range(size)])]
    ppermute x0 -> x22, starting transfers between devices: none -> 24 us  [flip(): return lax.ppermute(value, axis, [(i, i ^ mask) for i in range(size)])]
    pallas_call x0 -> x3, Pallas kernels: none -> 23.9 us  [the longest x2 22.9 us: hidden_terms(): pl.pallas_call(hidden_kernel, grid=(4, count), out_shape=jax.ShapeDtypeSt...]
    dot_general x4 -> x11, matrix products: 45.7 us -> 25.3 us  [dot(): lax.dot_general(lhs, rhs, (dims, ((), ())), preferred_element_type=jnp.fl...]
    unnamed x13 -> x35, local copies, waits for them, and re-layouts: 26.3 us -> 6.26 us
  transfers between devices with their start and end apart: 3 -> 26, of which waited for: 2 -> 14; matrix products, arithmetic and copies ran while one was open for 13% -> 29% of each run, Pallas kernels for 0% -> 11%
where the time goes in v1:
time: 216 us; the launch traced here: 214 us
  waiting for transfers between devices  58.1 us (27%)
  starting transfers between devices  48.4 us (22%)
  other arithmetic  33.1 us (15%)
  matrix products  25.3 us (12%)
  local copies, waits for them, and re-layouts  24.3 us (11%)
  Pallas kernels  23.9 us (11%)
    ppermute x22, waiting for transfers between devices, flip(): return lax.ppermute(value, axis, [(i, i ^ mask) for i in range(size)])  27.9 us
    dot_general x11, matrix products, dot(): lax.dot_general(lhs, rhs, (dims, ((), ())), preferred_element_type=jnp.fl...  25.3 us
    all_to_all x1, waiting for transfers between devices, local(): lax.all_to_all(grad_rows.reshape(owners_total, piece, quarter), SEQ, spli...  25.1 us
    ppermute x22, starting transfers between devices, flip(): return lax.ppermute(value, axis, [(i, i ^ mask) for i in range(size)])  24 us
    pallas_call x2, Pallas kernels, hidden_terms(): pl.pallas_call(hidden_kernel, grid=(4, count), out_shape=jax.ShapeDtypeSt...  22.9 us
    convert_element_type x13, other arithmetic, narrow(): return value.astype(jnp.bfloat16)  11.6 us
    all_to_all x2, starting transfers between devices, hidden_rest(): lax.all_to_all(terms, 'y', split_axis=0, concat_axis=0, tiled=True)  8.85 us
    all_to_all x1, starting transfers between devices, local(): lax.all_to_all(grad_rows.reshape(owners_total, piece, quarter), SEQ, spli...  8.32 us
  transfers between devices with their start and end apart: 26, of which 14 were waited for; matrix products, arithmetic and copies ran while one was open for 29% of the time, Pallas kernels for 11%

profile of v1, /device:TPU:8, one launch (start us, length us, event | category | flops | bytes accessed | tf_op | source)
XLA Modules:
  0.0 214.3 jit_solution(4529993770305905118)
XLA Ops:
  7.5 8.3 %all-to-all-start = ((bf16[32,16,2048]{2,1,0:T(8,128)(2,1)}), bf16[32,16,2048]{2,1,0:T(8,128)(2,1)S(1)}, u32[]{:S(2)}, u32[]{:S(2)}) async-start(bf16[32,16,2048]{2,1,0:T(8,128)(2,1)} %bitcast.143), calls=%async_computation | async-start | bytes 4194304 | tf_op jit(solution)/shard_map/all_to_all | solution.py:136
  20.7 25.1 %all-to-all-done.blocks_ref = bf16[32,16,2048]{2,1,0:T(8,128)(2,1)S(1)} async-done(((bf16[32,16,2048]{2,1,0:T(8,128)(2,1)}), bf16[32,16,2048]{2,1,0:T(8,128)(2,1)S(1)}, u32[]{:S(2)}, u32[]{:S(2)}) %all-to-all-start) | async-done | bytes 2097184 | tf_op jit(solution)/shard_map/all_to_all | solution.py:136
  58.1 7.3 %all-to-all-start.1 = ((bf16[32,16,2048]{2,1,0:T(8,128)(2,1)}), bf16[32,16,2048]{2,1,0:T(8,128)(2,1)S(1)}, u32[]{:S(2)}, u32[]{:S(2)}) async-start(bf16[32,16,2048]{2,1,0:T(8,128)(2,1)} %copy-done.2), calls=%async_computation.1 | async-start | bytes 4194304 | tf_op jit(solution)/shard_map/all_to_all | solution.py:143
  65.3 2.9 %collective-permute-done.3 = bf16[2,160,1024]{2,1,0:T(8,128)(2,1)} collective-permute-done((bf16[2,160,1024]{2,1,0:T(8,128)(2,1)}, bf16[2,160,1024]{2,1,0:T(8,128)(2,1)}, u32[]{:S(2)}, u32[]{:S(2)}) %collective-permute-start.3) | collective-permute-done | bytes 655392 | tf_op jit(solution)/shard_map/ppermute | solution.py:17
  68.2 3.9 %collective-permute-done.4 = bf16[2,160,1024]{2,1,0:T(8,128)(2,1)} collective-permute-done((bf16[2,160,1024]{2,1,0:T(8,128)(2,1)}, bf16[2,160,1024]{2,1,0:T(8,128)(2,1)}, u32[]{:S(2)}, u32[]{:S(2)}) %collective-permute-start.4) | collective-permute-done | bytes 655392 | tf_op jit(solution)/shard_map/ppermute | solution.py:17
  73.5 2.9 %pad_maximum_fusion = bf16[4,4,160,1024]{3,2,1,0:T(8,128)(2,1)S(1)} fusion(bf16[1,4,160,1024]{3,2,1,0:T(8,128)(2,1)} %bitcast.9, bf16[1,4,160,1024]{3,2,1,0:T(8,128)(2,1)S(1)} %maximum_bitcast_fusion.1, bf16[1,4,160,1024]{3,2,1,0:T(8,128)(2,1)} %bitcast.7, bf16[1,4,160,1024]{3,2,1,0:T(8,128)(2,1)S(1)} %copy-done.5), kind=kLoop, calls=%fused_computation.1 | loop fusion | flops 7864320 | bytes 10485760 | tf_op jit(solution)/shard_map/stack | solution.py:102
  85.8 4.4 %pad_maximum_fusion.5 = (bf16[2,4,160,1024]{3,2,1,0:T(8,128)(2,1)}, bf16[2,4,160,1024]{3,2,1,0:T(8,128)(2,1)}, bf16[2,4,160,1024]{3,2,1,0:T(8,128)(2,1)}, bf16[2,4,160,1024]{3,2,1,0:T(8,128)(2,1)}) fusion(bf16[1,4,160,1024]{3,2,1,0:T(8,128)(2,1)S(1)} %get-tuple-element.49, bf16[1,4,160,1024]{3,2,1,0:T(8,128)(2,1)S(1)} %get-tuple-element.46, ...), kind=kLoop, calls=%fused_computation.20 | loop fusion | flops 5242880 | bytes 15728640 | tf_op jit(solution)/shard_map/concatenate | solution.py:91
  90.2 5.1 %all-to-all-done.1 = bf16[32,16,2048]{2,1,0:T(8,128)(2,1)S(1)} async-done(((bf16[32,16,2048]{2,1,0:T(8,128)(2,1)}), bf16[32,16,2048]{2,1,0:T(8,128)(2,1)S(1)}, u32[]{:S(2)}, u32[]{:S(2)}) %all-to-all-start.1) | async-done | bytes 2097184 | tf_op jit(solution)/shard_map/all_to_all | solution.py:143
  95.3 3.3 %fusion.3 = f32[512,1280]{1,0:T(8,128)} fusion(f32[512,1280]{1,0:T(8,128)} %get-tuple-element.71), kind=kLoop, calls=%fused_computation.15 | loop fusion | flops 5242880 | bytes 5242880 | tf_op jit(solution)/shard_map/add | solution.py:23
  98.7 5.6 %shard_map.78 = bf16[4,512,256]{2,1,0:T(8,128)(2,1)} custom-call(bf16[512,2048]{1,0:T(8,128)(2,1)S(1)} %bitcast.123, bf16[5120,2048]{1,0:T(8,128)(2,1)} %weights_ref.1), custom_call_target="tpu_custom_call" | custom-call | flops 2147483648 | bytes 7340032 | tf_op jit(solution)/shard_map/pallas_call | solution.py:59
  104.3 3.8 %all-to-all-start.2 = ((bf16[4,512,256]{2,1,0:T(8,128)(2,1)}), bf16[4,512,256]{2,1,0:T(8,128)(2,1)S(1)}, u32[]{:S(2)}, u32[]{:S(2)}) async-start(bf16[4,512,256]{2,1,0:T(8,128)(2,1)} %shard_map.78), calls=%async_computation.2 | async-start | bytes 2097152 | tf_op jit(solution)/shard_map/all_to_all | solution.py:175
  110.6 2.6 %convolution_convert_fusion.4 = bf16[1280,512]{1,0:T(8,128)(2,1)} fusion(bf16[1280,1024]{1,0:T(8,128)(2,1)S(1)} %bitcast.142, bf16[1024,2048]{1,0:T(8,128)(2,1)S(1)} %constant_dynamic-update-slice_fusion), kind=kOutput, calls=%fused_computation.8 | convolution fusion | flops 1342832640 | bytes 4980736 | tf_op jit(solution)/shard_map/dot_general | solution.py:78
  114.2 2.6 %convolution_convert_fusion.5 = bf16[1280,512]{1,0:T(8,128)(2,1)} fusion(bf16[1280,1024]{1,0:T(8,128)(2,1)S(1)} %bitcast.134, bf16[1024,2048]{1,0:T(8,128)(2,1)S(1)} %constant_dynamic-update-slice_fusion), kind=kOutput, calls=%fused_computation.9 | convolution fusion | flops 1342832640 | bytes 4980736 | tf_op jit(solution)/shard_map/dot_general | solution.py:78
  116.8 2.7 %convolution_convert_fusion.6 = bf16[1280,512]{1,0:T(8,128)(2,1)} fusion(bf16[1280,1024]{1,0:T(8,128)(2,1)S(1)} %bitcast.141, bf16[1024,2048]{1,0:T(8,128)(2,1)S(1)} %constant_dynamic-update-slice_fusion), kind=kOutput, calls=%fused_computation.10 | convolution fusion | flops 1342832640 | bytes 4980736 | tf_op jit(solution)/shard_map/dot_general | solution.py:78
  119.5 2.6 %convolution_convert_fusion.7 = bf16[1280,512]{1,0:T(8,128)(2,1)} fusion(bf16[1280,1024]{1,0:T(8,128)(2,1)S(1)} %bitcast.133, bf16[1024,2048]{1,0:T(8,128)(2,1)S(1)} %constant_dynamic-update-slice_fusion), kind=kOutput, calls=%fused_computation.11 | convolution fusion | flops 1342832640 | bytes 4980736 | tf_op jit(solution)/shard_map/dot_general | solution.py:78
  125.7 17.3 %shard_map.79 = bf16[4,512,1024]{2,1,0:T(8,128)(2,1)S(1)} custom-call(bf16[512,2048]{1,0:T(8,128)(2,1)S(1)} %bitcast.125, bf16[5120,2048]{1,0:T(8,128)(2,1)} %weights_ref.1), custom_call_target="tpu_custom_call" | custom-call | flops 8589934592 | bytes 23068672 | tf_op jit(solution)/shard_map/pallas_call | solution.py:59
  145.0 2.6 %convolution_convert_fusion.3 = bf16[1280,512]{1,0:T(8,128)(2,1)} fusion(bf16[1280,1024]{1,0:T(8,128)(2,1)S(1)} %bitcast.131, bf16[1024,2048]{1,0:T(8,128)(2,1)S(1)} %constant_dynamic-update-slice_fusion), kind=kOutput, calls=%fused_computation.7 | convolution fusion | flops 1342832640 | bytes 4980736 | tf_op jit(solution)/shard_map/dot_general | solution.py:78
  147.6 2.6 %convolution_convert_fusion.2 = bf16[1280,512]{1,0:T(8,128)(2,1)} fusion(bf16[1280,1024]{1,0:T(8,128)(2,1)S(1)} %bitcast.140, bf16[1024,2048]{1,0:T(8,128)(2,1)S(1)} %constant_dynamic-update-slice_fusion), kind=kOutput, calls=%fused_computation.6 | convolution fusion | flops 1342832640 | bytes 4980736 | tf_op jit(solution)/shard_map/dot_general | solution.py:78
  151.8 5.1 %all-to-all-start.3 = ((bf16[4,512,1024]{2,1,0:T(8,128)(2,1)}), bf16[4,512,1024]{2,1,0:T(8,128)(2,1)}, u32[]{:S(2)}, u32[]{:S(2)}) async-start(bf16[4,512,1024]{2,1,0:T(8,128)(2,1)} %copy-done.3), calls=%async_computation.3 | async-start | bytes 8388608 | tf_op jit(solution)/shard_map/all_to_all | solution.py:175
  158.6 3.6 %convolution_convert_fusion = bf16[1280,512]{1,0:T(8,128)(2,1)S(1)} fusion(bf16[1280,1024]{1,0:T(8,128)(2,1)} %bitcast.139, bf16[1024,2048]{1,0:T(8,128)(2,1)} %copy-done.16), kind=kOutput, calls=%fused_computation.4 | convolution fusion | flops 1342832640 | bytes 4980736 | tf_op jit(solution)/shard_map/dot_general | solution.py:78
  173.9 8.3 %collective-permute-done.7 = bf16[4,160,512]{2,1,0:T(8,128)(2,1)S(1)} collective-permute-done((bf16[4,160,512]{2,1,0:T(8,128)(2,1)S(1)}, bf16[4,160,512]{2,1,0:T(8,128)(2,1)S(1)}, u32[]{:S(2)}, u32[]{:S(2)}) %collective-permute-start.7) | collective-permute-done | bytes 655392 | tf_op jit(solution)/shard_map/ppermute | solution.py:17
  198.3 4.0 %collective-permute-done.20 = bf16[2,160,512]{2,1,0:T(8,128)(2,1)S(1)} collective-permute-done((bf16[2,160,512]{2,1,0:T(8,128)(2,1)S(1)}, bf16[2,160,512]{2,1,0:T(8,128)(2,1)S(1)}, u32[]{:S(2)}, u32[]{:S(2)}) %collective-permute-start.20) | collective-permute-done | bytes 327712 | tf_op jit(solution)/shard_map/ppermute | solution.py:17
  204.2 3.5 %collective-permute-done.21 = bf16[160,512]{1,0:T(8,128)(2,1)S(1)} collective-permute-done((bf16[160,512]{1,0:T(8,128)(2,1)S(1)}, bf16[160,512]{1,0:T(8,128)(2,1)S(1)}, u32[]{:S(2)}, u32[]{:S(2)}) %collective-permute-start.21) | collective-permute-done | bytes 163872 | tf_op jit(solution)/shard_map/ppermute | solution.py:17
  208.8 3.6 %convert_reduce_fusion = f32[512,1024]{1,0:T(8,128)S(1)} fusion(bf16[4,512,1024]{2,1,0:T(8,128)(2,1)} %all-to-all-done.3), kind=kLoop, calls=%fused_computation | loop fusion | flops 3670016 | bytes 6291456 | tf_op jit(solution)/shard_map/reduce_sum | solution.py:176
  (135 shorter events, 79.4 us)
Async XLA Ops:
  7.5 8.3 %collective-permute-start = (bf16[4,160,512]{2,1,0:T(8,128)(2,1)}, bf16[4,160,512]{2,1,0:T(8,128)(2,1)S(1)}, u32[]{:S(2)}, u32[]{:S(2)}) collective-permute-start(bf16[4,160,512]{2,1,0:T(8,128)(2,1)} %get-tuple-element.65), channel_id=1, source_target_pairs={{0,4},{4,0},{1,5},{5,1},{2,6},{6,2},{3,7},{7,3},{8,12},{12,8},{9,1... | collective-permute-start | bytes 1966088 | tf_op jit(solution)/shard_map/ppermute | solution.py:17
  7.5 38.3 %all-to-all-start = ((bf16[32,16,2048]{2,1,0:T(8,128)(2,1)}), bf16[32,16,2048]{2,1,0:T(8,128)(2,1)S(1)}, u32[]{:S(2)}, u32[]{:S(2)}) async-start(bf16[32,16,2048]{2,1,0:T(8,128)(2,1)} %bitcast.143), calls=%async_computation | async-start | bytes 4194304 | tf_op jit(solution)/shard_map/all_to_all | solution.py:136
  17.7 31.3 %collective-permute-start.1 = (bf16[4,160,1024]{2,1,0:T(8,128)(2,1)}, bf16[4,160,1024]{2,1,0:T(8,128)(2,1)}, u32[]{:S(2)}, u32[]{:S(2)}) collective-permute-start(bf16[4,160,1024]{2,1,0:T(8,128)(2,1)} %get-tuple-element.63), channel_id=1, source_target_pairs={{0,1},{1,0},{2,3},{3,2},{4,5},{5,4},{6,7},{7,6},{8,9},{9,8},{10,11... | collective-permute-start | bytes 3932168 | tf_op jit(solution)/shard_map/ppermute | solution.py:17
  18.1 31.7 %collective-permute-start.2 = (bf16[4,160,1024]{2,1,0:T(8,128)(2,1)}, bf16[4,160,1024]{2,1,0:T(8,128)(2,1)}, u32[]{:S(2)}, u32[]{:S(2)}) collective-permute-start(bf16[4,160,1024]{2,1,0:T(8,128)(2,1)} %get-tuple-element.63), channel_id=1, source_target_pairs={{0,3},{1,2},{2,1},{3,0},{4,7},{5,6},{6,5},{7,4},{8,11},{9,10},{10,... | collective-permute-start | bytes 3932168 | tf_op jit(solution)/shard_map/ppermute | solution.py:17
  51.8 16.4 %collective-permute-start.3 = (bf16[2,160,1024]{2,1,0:T(8,128)(2,1)}, bf16[2,160,1024]{2,1,0:T(8,128)(2,1)}, u32[]{:S(2)}, u32[]{:S(2)}) collective-permute-start(bf16[2,160,1024]{2,1,0:T(8,128)(2,1)} %slice.165), channel_id=1, source_target_pairs={{0,3},{1,2},{2,1},{3,0},{4,7},{5,6},{6,5},{7,4},{8,11},{9,10},{10,... | collective-permute-start | bytes 1966088 | tf_op jit(solution)/shard_map/ppermute | solution.py:17
  55.5 16.6 %collective-permute-start.4 = (bf16[2,160,1024]{2,1,0:T(8,128)(2,1)}, bf16[2,160,1024]{2,1,0:T(8,128)(2,1)}, u32[]{:S(2)}, u32[]{:S(2)}) collective-permute-start(bf16[2,160,1024]{2,1,0:T(8,128)(2,1)} %slice.166), channel_id=1, source_target_pairs={{0,1},{1,0},{2,3},{3,2},{4,5},{5,4},{6,7},{7,6},{8,9},{9,8},{10,11... | collective-permute-start | bytes 1966088 | tf_op jit(solution)/shard_map/ppermute | solution.py:17
  58.1 37.2 %all-to-all-start.1 = ((bf16[32,16,2048]{2,1,0:T(8,128)(2,1)}), bf16[32,16,2048]{2,1,0:T(8,128)(2,1)S(1)}, u32[]{:S(2)}, u32[]{:S(2)}) async-start(bf16[32,16,2048]{2,1,0:T(8,128)(2,1)} %copy-done.2), calls=%async_computation.1 | async-start | bytes 4194304 | tf_op jit(solution)/shard_map/all_to_all | solution.py:143
  95.3 12.9 %collective-permute-start.5 = (bf16[512,2048]{1,0:T(8,128)(2,1)S(1)}, bf16[512,2048]{1,0:T(8,128)(2,1)}, u32[]{:S(2)}, u32[]{:S(2)}) collective-permute-start(bf16[512,2048]{1,0:T(8,128)(2,1)S(1)} %bitcast.122), channel_id=1, source_target_pairs={{0,4},{4,0},{1,5},{5,1},{2,6},{6,2},{3,7},{7,3},{8,12},{12,8},{9,1... | collective-permute-start | bytes 6291464 | tf_op jit(solution)/shard_map/ppermute | solution.py:17
  104.3 47.5 %all-to-all-start.2 = ((bf16[4,512,256]{2,1,0:T(8,128)(2,1)}), bf16[4,512,256]{2,1,0:T(8,128)(2,1)S(1)}, u32[]{:S(2)}, u32[]{:S(2)}) async-start(bf16[4,512,256]{2,1,0:T(8,128)(2,1)} %shard_map.78), calls=%async_computation.2 | async-start | bytes 2097152 | tf_op jit(solution)/shard_map/all_to_all | solution.py:175
  122.2 41.6 %collective-permute-start.6 = (bf16[2,4,160,512]{3,2,1,0:T(8,128)(2,1)}, bf16[2,4,160,512]{3,2,1,0:T(8,128)(2,1)}, u32[]{:S(2)}, u32[]{:S(2)}) collective-permute-start(bf16[2,4,160,512]{3,2,1,0:T(8,128)(2,1)} %bitcast.19), channel_id=1, source_target_pairs={{0,8},{8,0},{16,24},{24,16},{1,9},{9,1},{17,25},{25,17},{2,10},{10... | collective-permute-start | bytes 3932168 | tf_op jit(solution)/shard_map/ppermute | solution.py:17
  122.2 44.8 %collective-permute-start.10 = (bf16[2,4,160,512]{3,2,1,0:T(8,128)(2,1)}, bf16[2,4,160,512]{3,2,1,0:T(8,128)(2,1)}, u32[]{:S(2)}, u32[]{:S(2)}) collective-permute-start(bf16[2,4,160,512]{3,2,1,0:T(8,128)(2,1)} %bitcast.20), channel_id=1, source_target_pairs={{0,32},{32,0},{64,96},{96,64},{1,33},{33,1},{65,97},{97,65},{2,34}... | collective-permute-start | bytes 3932168 | tf_op jit(solution)/shard_map/ppermute | solution.py:17
  122.4 47.3 %collective-permute-start.14 = (bf16[2,4,160,512]{3,2,1,0:T(8,128)(2,1)}, bf16[2,4,160,512]{3,2,1,0:T(8,128)(2,1)}, u32[]{:S(2)}, u32[]{:S(2)}) collective-permute-start(bf16[2,4,160,512]{3,2,1,0:T(8,128)(2,1)} %bitcast.21), channel_id=1, source_target_pairs={{0,24},{8,16},{16,8},{24,0},{1,25},{9,17},{17,9},{25,1},{2,26},{10... | collective-permute-start | bytes 3932168 | tf_op jit(solution)/shard_map/ppermute | solution.py:17
  123.9 47.8 %collective-permute-start.18 = (bf16[2,4,160,512]{3,2,1,0:T(8,128)(2,1)}, bf16[2,4,160,512]{3,2,1,0:T(8,128)(2,1)}, u32[]{:S(2)}, u32[]{:S(2)}) collective-permute-start(bf16[2,4,160,512]{3,2,1,0:T(8,128)(2,1)} %bitcast.22), channel_id=1, source_target_pairs={{0,96},{32,64},{64,32},{96,0},{1,97},{33,65},{65,33},{97,1},{2,98}... | collective-permute-start | bytes 3932168 | tf_op jit(solution)/shard_map/ppermute | solution.py:17
  151.8 57.0 %all-to-all-start.3 = ((bf16[4,512,1024]{2,1,0:T(8,128)(2,1)}), bf16[4,512,1024]{2,1,0:T(8,128)(2,1)}, u32[]{:S(2)}, u32[]{:S(2)}) async-start(bf16[4,512,1024]{2,1,0:T(8,128)(2,1)} %copy-done.3), calls=%async_computation.3 | async-start | bytes 8388608 | tf_op jit(solution)/shard_map/all_to_all | solution.py:175
  165.1 17.0 %collective-permute-start.7 = (bf16[4,160,512]{2,1,0:T(8,128)(2,1)S(1)}, bf16[4,160,512]{2,1,0:T(8,128)(2,1)S(1)}, u32[]{:S(2)}, u32[]{:S(2)}) collective-permute-start(bf16[4,160,512]{2,1,0:T(8,128)(2,1)S(1)} %fusion.19), channel_id=1, source_target_pairs={{0,24},{8,16},{16,8},{24,0},{1,25},{9,17},{17,9},{25,1},{2,26},{10... | collective-permute-start | bytes 1966088 | tf_op jit(solution)/shard_map/ppermute | solution.py:17
  168.2 16.6 %collective-permute-start.11 = (bf16[4,160,512]{2,1,0:T(8,128)(2,1)S(1)}, bf16[4,160,512]{2,1,0:T(8,128)(2,1)S(1)}, u32[]{:S(2)}, u32[]{:S(2)}) collective-permute-start(bf16[4,160,512]{2,1,0:T(8,128)(2,1)S(1)} %fusion.16), channel_id=1, source_target_pairs={{0,96},{32,64},{64,32},{96,0},{1,97},{33,65},{65,33},{97,1},{2,98}... | collective-permute-start | bytes 1966088 | tf_op jit(solution)/shard_map/ppermute | solution.py:17
  171.0 15.9 %collective-permute-start.15 = (bf16[4,160,512]{2,1,0:T(8,128)(2,1)S(1)}, bf16[4,160,512]{2,1,0:T(8,128)(2,1)S(1)}, u32[]{:S(2)}, u32[]{:S(2)}) collective-permute-start(bf16[4,160,512]{2,1,0:T(8,128)(2,1)S(1)} %fusion.13), channel_id=1, source_target_pairs={{0,8},{8,0},{16,24},{24,16},{1,9},{9,1},{17,25},{25,17},{2,10},{10... | collective-permute-start | bytes 1966088 | tf_op jit(solution)/shard_map/ppermute | solution.py:17
  173.0 17.7 %collective-permute-start.19 = (bf16[4,160,512]{2,1,0:T(8,128)(2,1)S(1)}, bf16[4,160,512]{2,1,0:T(8,128)(2,1)S(1)}, u32[]{:S(2)}, u32[]{:S(2)}) collective-permute-start(bf16[4,160,512]{2,1,0:T(8,128)(2,1)S(1)} %fusion.10), channel_id=1, source_target_pairs={{0,32},{32,0},{64,96},{96,64},{1,33},{33,1},{65,97},{97,65},{2,34}... | collective-permute-start | bytes 1966088 | tf_op jit(solution)/shard_map/ppermute | solution.py:17
  183.5 11.9 %collective-permute-start.8 = (bf16[2,160,512]{2,1,0:T(8,128)(2,1)S(1)}, bf16[2,160,512]{2,1,0:T(8,128)(2,1)S(1)}, u32[]{:S(2)}, u32[]{:S(2)}) collective-permute-start(bf16[2,160,512]{2,1,0:T(8,128)(2,1)S(1)} %slice.229), channel_id=1, source_target_pairs={{0,32},{32,0},{64,96},{96,64},{1,33},{33,1},{65,97},{97,65},{2,34}... | collective-permute-start | bytes 983048 | tf_op jit(solution)/shard_map/ppermute | solution.py:17
  186.2 10.5 %collective-permute-start.12 = (bf16[2,160,512]{2,1,0:T(8,128)(2,1)S(1)}, bf16[2,160,512]{2,1,0:T(8,128)(2,1)S(1)}, u32[]{:S(2)}, u32[]{:S(2)}) collective-permute-start(bf16[2,160,512]{2,1,0:T(8,128)(2,1)S(1)} %slice.238), channel_id=1, source_target_pairs={{0,8},{8,0},{16,24},{24,16},{1,9},{9,1},{17,25},{25,17},{2,10},{10... | collective-permute-start | bytes 983048 | tf_op jit(solution)/shard_map/ppermute | solution.py:17
  188.3 9.9 %collective-permute-start.16 = (bf16[2,160,512]{2,1,0:T(8,128)(2,1)S(1)}, bf16[2,160,512]{2,1,0:T(8,128)(2,1)S(1)}, u32[]{:S(2)}, u32[]{:S(2)}) collective-permute-start(bf16[2,160,512]{2,1,0:T(8,128)(2,1)S(1)} %slice.247), channel_id=1, source_target_pairs={{0,96},{32,64},{64,32},{96,0},{1,97},{33,65},{65,33},{97,1},{2,98}... | collective-permute-start | bytes 983048 | tf_op jit(solution)/shard_map/ppermute | solution.py:17
  192.1 10.2 %collective-permute-start.20 = (bf16[2,160,512]{2,1,0:T(8,128)(2,1)S(1)}, bf16[2,160,512]{2,1,0:T(8,128)(2,1)S(1)}, u32[]{:S(2)}, u32[]{:S(2)}) collective-permute-start(bf16[2,160,512]{2,1,0:T(8,128)(2,1)S(1)} %slice.256), channel_id=1, source_target_pairs={{0,24},{8,16},{16,8},{24,0},{1,25},{9,17},{17,9},{25,1},{2,26},{10... | collective-permute-start | bytes 983048 | tf_op jit(solution)/shard_map/ppermute | solution.py:17
  195.5 7.3 %collective-permute-start.9 = (bf16[160,512]{1,0:T(8,128)(2,1)S(1)}, bf16[160,512]{1,0:T(8,128)(2,1)S(1)}, u32[]{:S(2)}, u32[]{:S(2)}) collective-permute-start(bf16[160,512]{1,0:T(8,128)(2,1)S(1)} %fusion.37), channel_id=1, source_target_pairs={{0,96},{32,64},{64,32},{96,0},{1,97},{33,65},{65,33},{97,1},{2,98}... | collective-permute-start | bytes 491528 | tf_op jit(solution)/shard_map/ppermute | solution.py:17
  196.8 7.3 %collective-permute-start.13 = (bf16[160,512]{1,0:T(8,128)(2,1)S(1)}, bf16[160,512]{1,0:T(8,128)(2,1)S(1)}, u32[]{:S(2)}, u32[]{:S(2)}) collective-permute-start(bf16[160,512]{1,0:T(8,128)(2,1)S(1)} %fusion.38), channel_id=1, source_target_pairs={{0,24},{8,16},{16,8},{24,0},{1,25},{9,17},{17,9},{25,1},{2,26},{10... | collective-permute-start | bytes 491528 | tf_op jit(solution)/shard_map/ppermute | solution.py:17
  (19 other events, 121.7 us)

commit v2 on v1

v2 whole, which is shorter than its diff:
```python
import functools
import math

import jax
import jax.numpy as jnp
from jax import lax
from jax.experimental import pallas as pl
from jax.experimental.pallas import tpu as pltpu
from jax.sharding import Mesh
from jax.sharding import PartitionSpec as P

FRAME = 64
SEQ = ("z", "x", "core")


def flip(value, axis, mask):
    size = lax.axis_size(axis)
    return lax.ppermute(value, axis, [(i, i ^ mask) for i in range(size)])


def gelu_parts(values):
    normal_cdf = 0.5 * (1.0 + lax.erf(values * 0.7071067811865476))
    density = jnp.exp(-0.5 * values * values) * 0.3989422804014327
    return (values * normal_cdf, normal_cdf + values * density)


def place_kernel(owner_ref, blocks_ref, out_ref, staged, sem):
    def move(i, carry):
        staged[owner_ref[i]] = blocks_ref[i]
        return carry

    lax.fori_loop(0, blocks_ref.shape[0], move, 0)
    copy = pltpu.make_async_copy(staged, out_ref, sem)
    copy.start()
    copy.wait()


def place(owner, blocks):
    return pl.pallas_call(
        place_kernel,
        out_shape=pltpu.HBM(blocks.shape, blocks.dtype),
        in_specs=[pl.BlockSpec(memory_space=pltpu.SMEM), pl.BlockSpec(memory_space=pltpu.VMEM)],
        out_specs=pl.BlockSpec(memory_space=pltpu.HBM),
        scratch_shapes=[pltpu.VMEM(blocks.shape, blocks.dtype), pltpu.SemaphoreType.DMA],
        compiler_params=pltpu.CompilerParams(vmem_limit_bytes=12 << 20),
        cost_estimate=pl.CostEstimate(
            flops=0, transcendentals=0, bytes_accessed=2 * blocks.size * blocks.dtype.itemsize
        ),
    )(owner, blocks)


def hidden_kernel(rows_ref, weights_ref, out_ref):
    part = weights_ref[...].reshape(-1, weights_ref.shape[-1])
    out_ref[0] = dot(rows_ref[...], part, ((1,), (1,))).astype(out_ref.dtype)


def hidden_terms(rows, weights, first, count):
    tokens, depth = rows.shape
    width = weights.shape[2]
    return pl.pallas_call(
        hidden_kernel,
        grid=(4,),
        out_shape=pltpu.HBM((4, tokens, count * width), jnp.bfloat16),
        in_specs=[
            pl.BlockSpec((tokens, depth), lambda d: (0, 0)),
            pl.BlockSpec((1, count, width, depth), lambda d: (d, first // count, 0, 0)),
        ],
        out_specs=pl.BlockSpec((1, tokens, count * width), lambda d: (d, 0, 0)),
        compiler_params=pltpu.CompilerParams(vmem_limit_bytes=18 << 20),
        cost_estimate=pl.CostEstimate(
            flops=8 * tokens * depth * count * width,
            transcendentals=0,
            bytes_accessed=2 * (tokens * depth + 4 * count * width * (depth + tokens)),
        ),
    )(rows, pltpu.with_memory_space_constraint(weights, pltpu.HBM))


def dot(lhs, rhs, dims):
    return lax.dot_general(lhs, rhs, (dims, ((), ())), preferred_element_type=jnp.float32)


def wide(value):
    return value.astype(jnp.float32)


def narrow(value):
    return value.astype(jnp.bfloat16)


def after(value, *others):
    return lax.optimization_barrier((value, *others))[0]


def gather_ring(value, other):
    half = value.shape[0] // 2
    low, high = value[:half], value[half:]
    first = flip(low, "y", 1), flip(high, "y", 3)
    low, high, one_low, three_high, other = lax.optimization_barrier((low, high, *first, other))
    two_low, two_high = flip(one_low, "y", 3), flip(three_high, "y", 1)
    return [value, one_low, flip(high, "y", 1), flip(low, "y", 3), three_high, two_low, two_high], other


PLANS = (("x", "z", 1), ("z", "x", 1), ("x", "z", 3), ("z", "x", 3))


def arrange_kernel(starts, order_ref, *refs):
    inputs, outputs = refs[: len(starts)], refs[-len(PLANS) :]
    step = pl.program_id(0)
    for k, start in enumerate(starts):
        stop = starts[k + 1] if k + 1 < len(starts) else 16

        @pl.when((step >= start) & (step < stop))
        def _(k=k):
            for out_ref in outputs:
                out_ref[...] = inputs[k][...]


def arrange(pieces, order, offset, before=()):
    starts, total = [], 0
    for piece in pieces:
        starts.append(total)
        total += piece.shape[0]
    block = (1, *pieces[0].shape[1:])

    def source(start, count):
        return lambda i, order: (jnp.clip(i - start, 0, count - 1), 0, 0)

    def target(first, near):
        lead = 3 if near == 1 else 2

        def index(i, order):
            place = lax.shift_right_logical(i + offset, 2)
            z, x = place ^ lax.shift_right_logical(place, 1) ^ order[0], i & 3
            major, minor = (x, z) if first == "x" else (z, x)
            return (((major + lead) & 3) * 4 + minor, 0, 0)

        return index

    size = total * block[1] * block[2] * 2
    return pl.pallas_call(
        functools.partial(arrange_kernel, starts),
        grid_spec=pltpu.PrefetchScalarGridSpec(
            num_scalar_prefetch=1,
            grid=(total,),
            in_specs=[pl.BlockSpec(block, source(s, p.shape[0])) for s, p in zip(starts, pieces)]
            + [pl.BlockSpec(memory_space=pltpu.HBM) for _ in before],
            out_specs=[pl.BlockSpec(block, target(first, near)) for first, _, near in PLANS],
        ),
        out_shape=[pltpu.HBM((16, *block[1:]), jnp.bfloat16) for _ in PLANS],
        input_output_aliases={1 + len(pieces) + i: i for i in range(len(before))},
        compiler_params=pltpu.CompilerParams(vmem_limit_bytes=8 << 20),
        cost_estimate=pl.CostEstimate(flops=0, transcendentals=0, bytes_accessed=5 * size),
    )(order, *pieces, *before)


def product(part, rhs):
    return narrow(dot(part, rhs, ((1,), (0,)))).reshape(2, 4, -1, rhs.shape[1])


SENT = {1: slice(1, 3), 3: slice(2, 4)}
HELD = {1: slice(3, 5), 3: slice(0, 2)}
OWN, FAR = {1: 1, 3: 0}, {1: 0, 3: 1}
OWN_SENT, FAR_SENT = {1: 0, 3: 1}, {1: 1, 3: 0}


def scatter_first(arrived, kept, axis, near):
    far = 4 - near
    arrived_far = flip(narrow(wide(kept[FAR[near]]) + wide(arrived[FAR_SENT[near]])), axis, far)
    return narrow(wide(kept[OWN[near]]) + wide(arrived[OWN_SENT[near]]) + wide(arrived_far))


def scatter_second(total, axis, near):
    far = 4 - near
    arrived = flip(total[SENT[near]], axis, near)
    arrived_far = flip(narrow(wide(total[far]) + wide(arrived[FAR_SENT[near]])), axis, far)
    return wide(total[0]) + wide(arrived[OWN_SENT[near]]) + wide(arrived_far)


def local(grad_rows, img_start, img_len, img_owner, pre_act, w_out):
    stripe, quarter = grad_rows.shape
    owners_total = lax.axis_size(SEQ)
    frames = stripe // FRAME
    here = lax.axis_index(SEQ)
    x, y, z, core = (lax.axis_index(a) for a in ("x", "y", "z", "core"))
    piece = stripe // owners_total

    spread = lax.all_to_all(
        grad_rows.reshape(owners_total, piece, quarter), SEQ, split_axis=0, concat_axis=0, tiled=True
    )

    images = owners_total * frames
    image_ids = jnp.arange(images, dtype=jnp.int32)
    slots = jnp.arange(stripe, dtype=jnp.int32)
    chosen_image = (image_ids % frames == (slots // FRAME)[:, None]) & (img_owner == here)
    packed = (img_start - image_ids * FRAME) * (2 * FRAME) + img_len
    packed = jnp.where(chosen_image, packed, 0).sum(axis=1)
    offset, length = packed // (2 * FRAME), packed % (2 * FRAME)
    target = jnp.where(slots % FRAME < length, slots + offset, -1)
    chosen = (target[:, None] == slots).astype(jnp.bfloat16)

    units = pre_act.shape[1]
    _, derivative = gelu_parts(dot(chosen, pre_act, ((0,), (0,))))
    activation, _ = gelu_parts(dot(pre_act, chosen, ((0,), (0,))))
    halves = narrow(activation).reshape(4, 2, units // 8, stripe)

    def half_of(which):
        shape = (1, 1, *halves.shape[2:])
        parts = [lax.dynamic_slice(halves, (x ^ m, which, 0, 0), shape)[:, 0] for m in range(4)]
        return jnp.concatenate(parts, axis=0)

    both = jnp.concatenate([half_of(core), flip(half_of(1 - core), "core", 1)], axis=2)
    pieces, spread = gather_ring(both, spread)
    order = (y ^ z).reshape(1)
    arranged = arrange(pieces[5:], order, 12, arrange(pieces[:5], order, 0))
    owners = img_owner.reshape(owners_total, frames)
    frame_here = here * piece // FRAME
    owner_here = lax.dynamic_index_in_dim(owners, frame_here, 1, keepdims=False)
    placed = place(owner_here, spread)
    rows = lax.all_to_all(placed, SEQ, split_axis=0, concat_axis=0, tiled=True).reshape(stripe, quarter)
    lhs = [part.reshape(-1, 2 * stripe) for part in arranged]
    weights = w_out.reshape(4, 5, units // 5, quarter)
    rows, weights, lhs, derivative = lax.optimization_barrier((rows, weights, lhs, derivative))

    cut = units * 4 // 5

    def exchange(terms):
        return lax.all_to_all(terms, "y", split_axis=0, concat_axis=0, tiled=True)

    def hidden_rest(arrived, start, stop):
        grad = narrow(wide(arrived).sum(axis=0) * derivative[:, start:stop])
        return narrow(dot(chosen, grad, ((1,), (0,))))

    early = hidden_terms(rows, weights, 4, 1)

    pair = jnp.concatenate([rows, flip(rows, "core", 1)], axis=0)
    span = quarter // 4
    columns = [pair[:, i * span : (i + 1) * span] for i in range(4)]
    terms = [product(part[: part.shape[0] // 2], c) for part, c in zip(lhs, columns)]
    landed = [flip(term, first, near) for (first, _, near), term in zip(PLANS, terms)]

    done = [term[0, 0, :8, :128] for term in terms]
    early = exchange(after(early, *done))
    late = hidden_terms(rows, after(weights, *done), 0, 4)
    lhs, early, _ = lax.optimization_barrier((lhs, early, late))
    late = exchange(late)
    kept = [product(part[part.shape[0] // 2 :], c) for part, c in zip(lhs, columns)]

    totals = [scatter_first(a, k, first, near) for a, k, (first, _, near) in zip(landed, kept, PLANS)]
    sums = [scatter_second(t, second, near) for t, (_, second, near) in zip(totals, PLANS)]
    factor = 1.0 / math.sqrt(owners_total * stripe)
    weight_grad = narrow(jnp.concatenate(sums, axis=1) * factor)
    parts = [hidden_rest(late, 0, cut), hidden_rest(early, cut, units)]
    pre_grad = jnp.concatenate(parts, axis=1)
    return (pre_grad, weight_grad)


def solution(mesh):
    grid = Mesh(mesh.devices.reshape(4, 4, 2, 4), ("z", "x", "core", "y"))
    return jax.shard_map(
        local,
        mesh=grid,
        in_specs=(P(SEQ, "y"), P(), P(), P(), P(SEQ, "y"), P(None, "y")),
        out_specs=(P(SEQ, "y"), P(SEQ, "y")),
        check_vma=False,
    )
```

time: 216 us -> 194 us (0.90)
  local copies, waits for them, and re-layouts: 24.3 us -> 6.03 us
  other arithmetic: 33.1 us -> 20.6 us
  Pallas kernels: 23.9 us -> 32.3 us
  starting transfers between devices: 48.4 us -> 53.7 us
  waiting for transfers between devices: 58.1 us -> 55.5 us
    ppermute x22 -> x24, waiting for transfers between devices: 27.9 us -> 50.4 us  [flip(): return lax.ppermute(value, axis, [(i, i ^ mask) for i in range(size)])]
    all_to_all x1, waiting for transfers between devices: 25.1 us -> 4.57 us  [local(): lax.all_to_all(grad_rows.reshape(owners_total, piece, quarter), SEQ, spli...]
    slice x7 -> x1, local copies, waits for them, and re-layouts: 11 us -> 0.96 us  [gather_ring(): low, high = (value[:half], value[half:])]
    pallas_call x3 -> x5, Pallas kernels: 23.9 us -> 32.3 us  [the longest x2 18.5 us: hidden_terms(): pl.pallas_call(hidden_kernel, grid=(4,), out_shape=pltpu.HBM((4, tokens,...]
    another operation x3 -> x0, other arithmetic: 6.12 us -> none  [gather_ring(): return jnp.stack([value, one, two, three])]
    ppermute x22 -> x24, starting transfers between devices: 24 us -> 29.4 us  [flip(): return lax.ppermute(value, axis, [(i, i ^ mask) for i in range(size)])]
    all_to_all x1, waiting for transfers between devices: 5.1 us -> 0.01 us  [local(): lax.all_to_all(placed, SEQ, split_axis=0, concat_axis=0, tiled=True)]
    concatenate x2, other arithmetic: 4.55 us -> 0.23 us  [the longest x1 0.15 us: local(): jnp.concatenate([half_of(core), flip(half_of(1 - core), 'core', 1)], axis=2)]
  transfers between devices with their start and end apart: 26 -> 28, of which waited for: 14 -> 16; matrix products, arithmetic and copies ran while one was open for 29% -> 20% of each run, Pallas kernels for 11% -> 15%
where the time goes in v2:
time: 194 us; the launch traced here: 193 us
  waiting for transfers between devices  55.5 us (29%)
  starting transfers between devices  53.7 us (28%)
  Pallas kernels  32.3 us (17%)
  matrix products  23.6 us (12%)
  other arithmetic  20.6 us (11%)
  local copies, waits for them, and re-layouts  6.03 us (3%)
    ppermute x24, waiting for transfers between devices, flip(): return lax.ppermute(value, axis, [(i, i ^ mask) for i in range(size)])  50.4 us
    ppermute x24, starting transfers between devices, flip(): return lax.ppermute(value, axis, [(i, i ^ mask) for i in range(size)])  29.4 us
    dot_general x11, matrix products, dot(): lax.dot_general(lhs, rhs, (dims, ((), ())), preferred_element_type=jnp.fl...  23.6 us
    pallas_call x2, Pallas kernels, hidden_terms(): pl.pallas_call(hidden_kernel, grid=(4,), out_shape=pltpu.HBM((4, tokens,...  18.5 us
    all_to_all x2, starting transfers between devices, exchange(): return lax.all_to_all(terms, 'y', split_axis=0, concat_axis=0, tiled=True)  11.9 us
    convert_element_type x13, other arithmetic, narrow(): return value.astype(jnp.bfloat16)  11.6 us
    pallas_call x2, Pallas kernels, arrange(): pl.pallas_call(functools.partial(arrange_kernel, starts), grid_spec=pltpu...  10.5 us
    all_to_all x1, starting transfers between devices, local(): lax.all_to_all(grad_rows.reshape(owners_total, piece, quarter), SEQ, spli...  8.43 us
  transfers between devices with their start and end apart: 28, of which 16 were waited for; matrix products, arithmetic and copies ran while one was open for 20% of the time, Pallas kernels for 15%

profile of v2, /device:TPU:8, one launch (start us, length us, event | category | flops | bytes accessed | tf_op | source)
XLA Modules:
  0.0 193.0 jit_solution(12321276341586457845)
XLA Ops:
  0.7 8.4 %all-to-all-start = ((bf16[32,16,2048]{2,1,0:T(8,128)(2,1)}), bf16[32,16,2048]{2,1,0:T(8,128)(2,1)}, u32[]{:S(2)}, u32[]{:S(2)}) async-start(bf16[32,16,2048]{2,1,0:T(8,128)(2,1)} %bitcast.158), calls=%async_computation | async-start | bytes 4194304 | tf_op jit(solution)/shard_map/all_to_all | solution.py:187
  9.5 2.6 %fusion.15 = (bf16[1280,512]{0,1:T(8,128)(2,1)S(1)}, f32[512,1280]{1,0:T(8,128)}) fusion(bf16[512,1280]{1,0:T(8,128)(2,1)S(1)} %copy-done, s32[512]{0:T(512)S(1)} %fusion.48), kind=kOutput, calls=%fused_computation.27 | convolution fusion | flops 674627584 | bytes 5244928 | tf_op jit(solution)/shard_map/dot_general | solution.py:79
  20.0 13.3 %collective-permute-done.2.refs_4_ = bf16[2,160,1024]{2,1,0:T(8,128)(2,1)S(1)} collective-permute-done((bf16[2,160,1024]{2,1,0:T(8,128)(2,1)}, bf16[2,160,1024]{2,1,0:T(8,128)(2,1)S(1)}, u32[]{:S(2)}, u32[]{:S(2)}) %collective-permute-start.2) | collective-permute-done | bytes 655392 | tf_op jit(solution)/shard_map/ppermute | solution.py:18
  34.5 4.6 %all-to-all-done.blocks_ref = bf16[32,16,2048]{2,1,0:T(8,128)(2,1)} async-done(((bf16[32,16,2048]{2,1,0:T(8,128)(2,1)}), bf16[32,16,2048]{2,1,0:T(8,128)(2,1)}, u32[]{:S(2)}, u32[]{:S(2)}) %all-to-all-start) | async-done | bytes 2097184 | tf_op jit(solution)/shard_map/all_to_all | solution.py:187
  39.1 3.3 %shard_map.77 = bf16[32,16,2048]{2,1,0:T(8,128)(2,1)} custom-call(s32[32]{0:T(128)S(1)} %dynamic-slice_reduce_fusion.owner_ref, bf16[32,16,2048]{2,1,0:T(8,128)(2,1)} %all-to-all-done.blocks_ref), custom_call_target="tpu_custom_call" | custom-call | bytes 4194304 | tf_op jit(solution)/shard_map/pallas_call | solution.py:39
  42.4 4.0 %all-to-all-start.1 = ((bf16[32,16,2048]{2,1,0:T(8,128)(2,1)}), bf16[32,16,2048]{2,1,0:T(8,128)(2,1)S(1)}, u32[]{:S(2)}, u32[]{:S(2)}) async-start(bf16[32,16,2048]{2,1,0:T(8,128)(2,1)} %shard_map.77), calls=%async_computation.1 | async-start | bytes 4194304 | tf_op jit(solution)/shard_map/all_to_all | solution.py:219
  51.8 3.4 %fusion.3 = f32[512,1280]{1,0:T(8,128)} fusion(f32[512,1280]{1,0:T(8,128)} %get-tuple-element.75), kind=kLoop, calls=%fused_computation.13 | loop fusion | flops 5242880 | bytes 5242880 | tf_op jit(solution)/shard_map/add | solution.py:24
  55.2 9.1 %collective-permute-done.5.refs_2_ = bf16[2,160,1024]{2,1,0:T(8,128)(2,1)S(1)} collective-permute-done((bf16[2,160,1024]{2,1,0:T(8,128)(2,1)}, bf16[2,160,1024]{2,1,0:T(8,128)(2,1)S(1)}, u32[]{:S(2)}, u32[]{:S(2)}) %collective-permute-start.5) | collective-permute-done | bytes 655392 | tf_op jit(solution)/shard_map/ppermute | solution.py:18
  65.1 7.7 %shard_map.78 = (bf16[16,160,1024]{2,1,0:T(8,128)(2,1)}, bf16[16,160,1024]{2,1,0:T(8,128)(2,1)}, bf16[16,160,1024]{2,1,0:T(8,128)(2,1)}, bf16[16,160,1024]{2,1,0:T(8,128)(2,1)}) custom-call(s32[1]{0:T(128)} %bitcast.13.order_ref, bf16[4,160,1024]{2,1,0:T(8,128)(2,1)S(1)} %pad_maximum_fusion.refs_0_, bf16[2,160,1024]{2,1,0:T(8,128)(2,1)S(1)} %copy-done.5, ...), custom_call_target="tpu_custom_call" | custom-call | bytes 19660800 | tf_op jit(solution)/shard_map/pallas_call | solution.py:140
  72.9 5.5 %collective-permute-done.3.refs_0_ = bf16[2,160,1024]{2,1,0:T(8,128)(2,1)S(1)} collective-permute-done((bf16[2,160,1024]{2,1,0:T(8,128)(2,1)}, bf16[2,160,1024]{2,1,0:T(8,128)(2,1)S(1)}, u32[]{:S(2)}, u32[]{:S(2)}) %collective-permute-start.3) | collective-permute-done | bytes 655392 | tf_op jit(solution)/shard_map/ppermute | solution.py:18
  78.4 2.8 %shard_map.79 = (bf16[16,160,1024]{2,1,0:T(8,128)(2,1)}, bf16[16,160,1024]{2,1,0:T(8,128)(2,1)}, bf16[16,160,1024]{2,1,0:T(8,128)(2,1)}, bf16[16,160,1024]{2,1,0:T(8,128)(2,1)}) custom-call(s32[1]{0:T(128)} %bitcast.13.order_ref, ...), custom_call_target="tpu_custom_call", output_to_operand_aliasing={{0}: (3, {}), {1}: (4, {}), {2}: (5, {}), {3}: (6, {})} | custom-call | bytes 6553600 | tf_op jit(solution)/shard_map/pallas_call | solution.py:140
  81.2 5.6 %shard_map.81 = bf16[4,512,256]{2,1,0:T(8,128)(2,1)} custom-call(bf16[512,2048]{1,0:T(8,128)(2,1)S(1)} %bitcast.124, bf16[4,5,256,2048]{3,2,1,0:T(8,128)(2,1)} %bitcast.127), custom_call_target="tpu_custom_call" | custom-call | flops 2147483648 | bytes 7340032 | tf_op jit(solution)/shard_map/pallas_call | solution.py:60
  89.3 2.6 %convolution_convert_fusion.7 = bf16[1280,512]{1,0:T(8,128)(2,1)} fusion(bf16[2560,1024]{1,0:T(8,128)(2,1)S(1)} %bitcast.131, bf16[1024,2048]{1,0:T(8,128)(2,1)S(1)} %constant_dynamic-update-slice_fusion), kind=kOutput, calls=%fused_computation.9 | convolution fusion | flops 1342832640 | bytes 4980736 | tf_op jit(solution)/shard_map/dot_general | solution.py:79
  93.6 2.6 %convolution_convert_fusion.6 = bf16[1280,512]{1,0:T(8,128)(2,1)} fusion(bf16[2560,1024]{1,0:T(8,128)(2,1)S(1)} %bitcast.134, bf16[1024,2048]{1,0:T(8,128)(2,1)S(1)} %constant_dynamic-update-slice_fusion), kind=kOutput, calls=%fused_computation.8 | convolution fusion | flops 1342832640 | bytes 4980736 | tf_op jit(solution)/shard_map/dot_general | solution.py:79
  97.9 2.6 %convolution_convert_fusion.5 = bf16[1280,512]{1,0:T(8,128)(2,1)} fusion(bf16[2560,1024]{1,0:T(8,128)(2,1)S(1)} %bitcast.140, bf16[1024,2048]{1,0:T(8,128)(2,1)S(1)} %constant_dynamic-update-slice_fusion), kind=kOutput, calls=%fused_computation.7 | convolution fusion | flops 1342832640 | bytes 4980736 | tf_op jit(solution)/shard_map/dot_general | solution.py:79
  102.6 2.6 %convolution_convert_fusion.4 = bf16[1280,512]{1,0:T(8,128)(2,1)} fusion(bf16[2560,1024]{1,0:T(8,128)(2,1)S(1)} %bitcast.146, bf16[1024,2048]{1,0:T(8,128)(2,1)S(1)} %constant_dynamic-update-slice_fusion), kind=kOutput, calls=%fused_computation.6 | convolution fusion | flops 1342832640 | bytes 4980736 | tf_op jit(solution)/shard_map/dot_general | solution.py:79
  107.1 5.6 %all-to-all-start.3 = ((bf16[4,512,256]{2,1,0:T(8,128)(2,1)}), bf16[4,512,256]{2,1,0:T(8,128)(2,1)S(1)}, u32[]{:S(2)}, u32[]{:S(2)}) async-start(bf16[4,512,256]{2,1,0:T(8,128)(2,1)} %shard_map.81), calls=%async_computation.3 | async-start | bytes 2097152 | tf_op jit(solution)/shard_map/all_to_all | solution.py:227
  112.7 13.0 %shard_map.80 = bf16[4,512,1024]{2,1,0:T(8,128)(2,1)} custom-call(bf16[512,2048]{1,0:T(8,128)(2,1)S(1)} %bitcast.126, bf16[4,5,256,2048]{3,2,1,0:T(8,128)(2,1)} %bitcast.128), custom_call_target="tpu_custom_call" | custom-call | flops 8589934592 | bytes 23068672 | tf_op jit(solution)/shard_map/pallas_call | solution.py:60
  126.2 6.2 %all-to-all-start.2 = ((bf16[4,512,1024]{2,1,0:T(8,128)(2,1)}), bf16[4,512,1024]{2,1,0:T(8,128)(2,1)}, u32[]{:S(2)}, u32[]{:S(2)}) async-start(bf16[4,512,1024]{2,1,0:T(8,128)(2,1)} %shard_map.80), calls=%async_computation.2 | async-start | bytes 8388608 | tf_op jit(solution)/shard_map/all_to_all | solution.py:227
  132.6 3.7 %convolution_convert_fusion.3 = bf16[1280,512]{1,0:T(8,128)(2,1)S(1)} fusion(bf16[2560,1024]{1,0:T(8,128)(2,1)} %bitcast.130, bf16[1024,2048]{1,0:T(8,128)(2,1)} %copy-done.8), kind=kOutput, calls=%fused_computation.5 | convolution fusion | flops 1342832640 | bytes 4980736 | tf_op jit(solution)/shard_map/dot_general | solution.py:79
  151.9 9.4 %collective-permute-done.9 = bf16[4,160,512]{2,1,0:T(8,128)(2,1)S(1)} collective-permute-done((bf16[4,160,512]{2,1,0:T(8,128)(2,1)S(1)}, bf16[4,160,512]{2,1,0:T(8,128)(2,1)S(1)}, u32[]{:S(2)}, u32[]{:S(2)}) %collective-permute-start.9) | collective-permute-done | bytes 655392 | tf_op jit(solution)/shard_map/ppermute | solution.py:18
  177.7 3.3 %collective-permute-done.22 = bf16[2,160,512]{2,1,0:T(8,128)(2,1)S(1)} collective-permute-done((bf16[2,160,512]{2,1,0:T(8,128)(2,1)S(1)}, bf16[2,160,512]{2,1,0:T(8,128)(2,1)S(1)}, u32[]{:S(2)}, u32[]{:S(2)}) %collective-permute-start.22) | collective-permute-done | bytes 327712 | tf_op jit(solution)/shard_map/ppermute | solution.py:18
  183.1 3.4 %collective-permute-done.23 = bf16[160,512]{1,0:T(8,128)(2,1)S(1)} collective-permute-done((bf16[160,512]{1,0:T(8,128)(2,1)S(1)}, bf16[160,512]{1,0:T(8,128)(2,1)S(1)}, u32[]{:S(2)}, u32[]{:S(2)}) %collective-permute-start.23) | collective-permute-done | bytes 163872 | tf_op jit(solution)/shard_map/ppermute | solution.py:18
  187.5 3.6 %convert_reduce_fusion = f32[512,1024]{1,0:T(8,128)S(1)} fusion(bf16[4,512,1024]{2,1,0:T(8,128)(2,1)} %all-to-all-done.2), kind=kLoop, calls=%fused_computation | loop fusion | flops 3670016 | bytes 6291456 | tf_op jit(solution)/shard_map/reduce_sum | solution.py:230
  (149 shorter events, 62.8 us)
Async XLA Ops:
  0.7 38.4 %all-to-all-start = ((bf16[32,16,2048]{2,1,0:T(8,128)(2,1)}), bf16[32,16,2048]{2,1,0:T(8,128)(2,1)}, u32[]{:S(2)}, u32[]{:S(2)}) async-start(bf16[32,16,2048]{2,1,0:T(8,128)(2,1)} %bitcast.158), calls=%async_computation | async-start | bytes 4194304 | tf_op jit(solution)/shard_map/all_to_all | solution.py:187
  16.2 17.0 %collective-permute-start.2 = (bf16[2,160,1024]{2,1,0:T(8,128)(2,1)}, bf16[2,160,1024]{2,1,0:T(8,128)(2,1)S(1)}, u32[]{:S(2)}, u32[]{:S(2)}) collective-permute-start(bf16[2,160,1024]{2,1,0:T(8,128)(2,1)} %get-tuple-element.32), channel_id=1, source_target_pairs={{0,3},{1,2},{2,1},{3,0},{4,7},{5,6},{6,5},{7,4},{8,11},{9,10},{10,... | collective-permute-start | bytes 1966088 | tf_op jit(solution)/shard_map/ppermute | solution.py:18
  17.8 16.7 %collective-permute-start.1 = (bf16[2,160,1024]{2,1,0:T(8,128)(2,1)S(1)}, bf16[2,160,1024]{2,1,0:T(8,128)(2,1)S(1)}, u32[]{:S(2)}, u32[]{:S(2)}) collective-permute-start(bf16[2,160,1024]{2,1,0:T(8,128)(2,1)S(1)} %get-tuple-element.33), channel_id=1, source_target_pairs={{0,1},{1,0},{2,3},{3,2},{4,5},{5,4},{6,7},{7,6},{8,9},{9,8},{10,11... | collective-permute-start | bytes 1966088 | tf_op jit(solution)/shard_map/ppermute | solution.py:18
  42.4 38.8 %all-to-all-start.1 = ((bf16[32,16,2048]{2,1,0:T(8,128)(2,1)}), bf16[32,16,2048]{2,1,0:T(8,128)(2,1)S(1)}, u32[]{:S(2)}, u32[]{:S(2)}) async-start(bf16[32,16,2048]{2,1,0:T(8,128)(2,1)} %shard_map.77), calls=%async_computation.1 | async-start | bytes 4194304 | tf_op jit(solution)/shard_map/all_to_all | solution.py:219
  46.4 17.9 %collective-permute-start.5 = (bf16[2,160,1024]{2,1,0:T(8,128)(2,1)}, bf16[2,160,1024]{2,1,0:T(8,128)(2,1)S(1)}, u32[]{:S(2)}, u32[]{:S(2)}) collective-permute-start(bf16[2,160,1024]{2,1,0:T(8,128)(2,1)} %get-tuple-element.32), channel_id=1, source_target_pairs={{0,1},{1,0},{2,3},{3,2},{4,5},{5,4},{6,7},{7,6},{8,9},{9,8},{10,11... | collective-permute-start | bytes 1966088 | tf_op jit(solution)/shard_map/ppermute | solution.py:18
  47.2 18.0 %collective-permute-start.6 = (bf16[2,160,1024]{2,1,0:T(8,128)(2,1)}, bf16[2,160,1024]{2,1,0:T(8,128)(2,1)S(1)}, u32[]{:S(2)}, u32[]{:S(2)}) collective-permute-start(bf16[2,160,1024]{2,1,0:T(8,128)(2,1)} %copy-done.10), channel_id=1, source_target_pairs={{0,3},{1,2},{2,1},{3,0},{4,7},{5,6},{6,5},{7,4},{8,11},{9,10},{10,... | collective-permute-start | bytes 1966088 | tf_op jit(solution)/shard_map/ppermute | solution.py:18
  49.4 29.0 %collective-permute-start.3 = (bf16[2,160,1024]{2,1,0:T(8,128)(2,1)}, bf16[2,160,1024]{2,1,0:T(8,128)(2,1)S(1)}, u32[]{:S(2)}, u32[]{:S(2)}) collective-permute-start(bf16[2,160,1024]{2,1,0:T(8,128)(2,1)} %copy-done.4), channel_id=1, source_target_pairs={{0,3},{1,2},{2,1},{3,0},{4,7},{5,6},{6,5},{7,4},{8,11},{9,10},{10,... | collective-permute-start | bytes 1966088 | tf_op jit(solution)/shard_map/ppermute | solution.py:18
  49.4 29.0 %collective-permute-start.4 = (bf16[2,160,1024]{2,1,0:T(8,128)(2,1)}, bf16[2,160,1024]{2,1,0:T(8,128)(2,1)S(1)}, u32[]{:S(2)}, u32[]{:S(2)}) collective-permute-start(bf16[2,160,1024]{2,1,0:T(8,128)(2,1)} %copy-done.2), channel_id=1, source_target_pairs={{0,1},{1,0},{2,3},{3,2},{4,5},{5,4},{6,7},{7,6},{8,9},{9,8},{10,11... | collective-permute-start | bytes 1966088 | tf_op jit(solution)/shard_map/ppermute | solution.py:18
  91.9 52.0 %collective-permute-start.8 = (bf16[2,4,160,512]{3,2,1,0:T(8,128)(2,1)}, bf16[2,4,160,512]{3,2,1,0:T(8,128)(2,1)}, u32[]{:S(2)}, u32[]{:S(2)}) collective-permute-start(bf16[2,4,160,512]{3,2,1,0:T(8,128)(2,1)} %bitcast.18), channel_id=1, source_target_pairs={{0,8},{8,0},{16,24},{24,16},{1,9},{9,1},{17,25},{25,17},{2,10},{10... | collective-permute-start | bytes 3932168 | tf_op jit(solution)/shard_map/ppermute | solution.py:18
  96.2 50.2 %collective-permute-start.12 = (bf16[2,4,160,512]{3,2,1,0:T(8,128)(2,1)}, bf16[2,4,160,512]{3,2,1,0:T(8,128)(2,1)}, u32[]{:S(2)}, u32[]{:S(2)}) collective-permute-start(bf16[2,4,160,512]{3,2,1,0:T(8,128)(2,1)} %bitcast.20), channel_id=1, source_target_pairs={{0,32},{32,0},{64,96},{96,64},{1,33},{33,1},{65,97},{97,65},{2,34}... | collective-permute-start | bytes 3932168 | tf_op jit(solution)/shard_map/ppermute | solution.py:18
  100.5 48.7 %collective-permute-start.16 = (bf16[2,4,160,512]{3,2,1,0:T(8,128)(2,1)}, bf16[2,4,160,512]{3,2,1,0:T(8,128)(2,1)}, u32[]{:S(2)}, u32[]{:S(2)}) collective-permute-start(bf16[2,4,160,512]{3,2,1,0:T(8,128)(2,1)} %bitcast.22), channel_id=1, source_target_pairs={{0,24},{8,16},{16,8},{24,0},{1,25},{9,17},{17,9},{25,1},{2,26},{10... | collective-permute-start | bytes 3932168 | tf_op jit(solution)/shard_map/ppermute | solution.py:18
  105.2 45.4 %collective-permute-start.20 = (bf16[2,4,160,512]{3,2,1,0:T(8,128)(2,1)}, bf16[2,4,160,512]{3,2,1,0:T(8,128)(2,1)}, u32[]{:S(2)}, u32[]{:S(2)}) collective-permute-start(bf16[2,4,160,512]{3,2,1,0:T(8,128)(2,1)} %bitcast.24), channel_id=1, source_target_pairs={{0,96},{32,64},{64,32},{96,0},{1,97},{33,65},{65,33},{97,1},{2,98}... | collective-permute-start | bytes 3932168 | tf_op jit(solution)/shard_map/ppermute | solution.py:18
  107.1 19.1 %all-to-all-start.3 = ((bf16[4,512,256]{2,1,0:T(8,128)(2,1)}), bf16[4,512,256]{2,1,0:T(8,128)(2,1)S(1)}, u32[]{:S(2)}, u32[]{:S(2)}) async-start(bf16[4,512,256]{2,1,0:T(8,128)(2,1)} %shard_map.81), calls=%async_computation.3 | async-start | bytes 2097152 | tf_op jit(solution)/shard_map/all_to_all | solution.py:227
  126.2 61.3 %all-to-all-start.2 = ((bf16[4,512,1024]{2,1,0:T(8,128)(2,1)}), bf16[4,512,1024]{2,1,0:T(8,128)(2,1)}, u32[]{:S(2)}, u32[]{:S(2)}) async-start(bf16[4,512,1024]{2,1,0:T(8,128)(2,1)} %shard_map.80), calls=%async_computation.2 | async-start | bytes 8388608 | tf_op jit(solution)/shard_map/all_to_all | solution.py:227
  145.2 16.1 %collective-permute-start.9 = (bf16[4,160,512]{2,1,0:T(8,128)(2,1)S(1)}, bf16[4,160,512]{2,1,0:T(8,128)(2,1)S(1)}, u32[]{:S(2)}, u32[]{:S(2)}) collective-permute-start(bf16[4,160,512]{2,1,0:T(8,128)(2,1)S(1)} %fusion.26), channel_id=1, source_target_pairs={{0,24},{8,16},{16,8},{24,0},{1,25},{9,17},{17,9},{25,1},{2,26},{10... | collective-permute-start | bytes 1966088 | tf_op jit(solution)/shard_map/ppermute | solution.py:18
  147.7 16.0 %collective-permute-start.13 = (bf16[4,160,512]{2,1,0:T(8,128)(2,1)S(1)}, bf16[4,160,512]{2,1,0:T(8,128)(2,1)S(1)}, u32[]{:S(2)}, u32[]{:S(2)}) collective-permute-start(bf16[4,160,512]{2,1,0:T(8,128)(2,1)S(1)} %fusion.23), channel_id=1, source_target_pairs={{0,96},{32,64},{64,32},{96,0},{1,97},{33,65},{65,33},{97,1},{2,98}... | collective-permute-start | bytes 1966088 | tf_op jit(solution)/shard_map/ppermute | solution.py:18
  150.4 14.8 %collective-permute-start.17 = (bf16[4,160,512]{2,1,0:T(8,128)(2,1)S(1)}, bf16[4,160,512]{2,1,0:T(8,128)(2,1)S(1)}, u32[]{:S(2)}, u32[]{:S(2)}) collective-permute-start(bf16[4,160,512]{2,1,0:T(8,128)(2,1)S(1)} %fusion.20), channel_id=1, source_target_pairs={{0,8},{8,0},{16,24},{24,16},{1,9},{9,1},{17,25},{25,17},{2,10},{10... | collective-permute-start | bytes 1966088 | tf_op jit(solution)/shard_map/ppermute | solution.py:18
  151.8 17.7 %collective-permute-start.21 = (bf16[4,160,512]{2,1,0:T(8,128)(2,1)S(1)}, bf16[4,160,512]{2,1,0:T(8,128)(2,1)S(1)}, u32[]{:S(2)}, u32[]{:S(2)}) collective-permute-start(bf16[4,160,512]{2,1,0:T(8,128)(2,1)S(1)} %fusion.17), channel_id=1, source_target_pairs={{0,32},{32,0},{64,96},{96,64},{1,33},{33,1},{65,97},{97,65},{2,34}... | collective-permute-start | bytes 1966088 | tf_op jit(solution)/shard_map/ppermute | solution.py:18
  162.7 10.5 %collective-permute-start.10 = (bf16[2,160,512]{2,1,0:T(8,128)(2,1)S(1)}, bf16[2,160,512]{2,1,0:T(8,128)(2,1)S(1)}, u32[]{:S(2)}, u32[]{:S(2)}) collective-permute-start(bf16[2,160,512]{2,1,0:T(8,128)(2,1)S(1)} %slice.247), channel_id=1, source_target_pairs={{0,32},{32,0},{64,96},{96,64},{1,33},{33,1},{65,97},{97,65},{2,34}... | collective-permute-start | bytes 983048 | tf_op jit(solution)/shard_map/ppermute | solution.py:18
  165.2 10.2 %collective-permute-start.14 = (bf16[2,160,512]{2,1,0:T(8,128)(2,1)S(1)}, bf16[2,160,512]{2,1,0:T(8,128)(2,1)S(1)}, u32[]{:S(2)}, u32[]{:S(2)}) collective-permute-start(bf16[2,160,512]{2,1,0:T(8,128)(2,1)S(1)} %slice.256), channel_id=1, source_target_pairs={{0,8},{8,0},{16,24},{24,16},{1,9},{9,1},{17,25},{25,17},{2,10},{10... | collective-permute-start | bytes 983048 | tf_op jit(solution)/shard_map/ppermute | solution.py:18
  166.6 10.9 %collective-permute-start.18 = (bf16[2,160,512]{2,1,0:T(8,128)(2,1)S(1)}, bf16[2,160,512]{2,1,0:T(8,128)(2,1)S(1)}, u32[]{:S(2)}, u32[]{:S(2)}) collective-permute-start(bf16[2,160,512]{2,1,0:T(8,128)(2,1)S(1)} %slice.265), channel_id=1, source_target_pairs={{0,96},{32,64},{64,32},{96,0},{1,97},{33,65},{65,33},{97,1},{2,98}... | collective-permute-start | bytes 983048 | tf_op jit(solution)/shard_map/ppermute | solution.py:18
  170.9 10.1 %collective-permute-start.22 = (bf16[2,160,512]{2,1,0:T(8,128)(2,1)S(1)}, bf16[2,160,512]{2,1,0:T(8,128)(2,1)S(1)}, u32[]{:S(2)}, u32[]{:S(2)}) collective-permute-start(bf16[2,160,512]{2,1,0:T(8,128)(2,1)S(1)} %slice.274), channel_id=1, source_target_pairs={{0,24},{8,16},{16,8},{24,0},{1,25},{9,17},{17,9},{25,1},{2,26},{10... | collective-permute-start | bytes 983048 | tf_op jit(solution)/shard_map/ppermute | solution.py:18
  173.2 8.3 %collective-permute-start.11 = (bf16[160,512]{1,0:T(8,128)(2,1)S(1)}, bf16[160,512]{1,0:T(8,128)(2,1)S(1)}, u32[]{:S(2)}, u32[]{:S(2)}) collective-permute-start(bf16[160,512]{1,0:T(8,128)(2,1)S(1)} %fusion.41), channel_id=1, source_target_pairs={{0,96},{32,64},{64,32},{96,0},{1,97},{33,65},{65,33},{97,1},{2,98}... | collective-permute-start | bytes 491528 | tf_op jit(solution)/shard_map/ppermute | solution.py:18
  175.4 7.4 %collective-permute-start.15 = (bf16[160,512]{1,0:T(8,128)(2,1)S(1)}, bf16[160,512]{1,0:T(8,128)(2,1)S(1)}, u32[]{:S(2)}, u32[]{:S(2)}) collective-permute-start(bf16[160,512]{1,0:T(8,128)(2,1)S(1)} %fusion.42), channel_id=1, source_target_pairs={{0,24},{8,16},{16,8},{24,0},{1,25},{9,17},{17,9},{25,1},{2,26},{10... | collective-permute-start | bytes 491528 | tf_op jit(solution)/shard_map/ppermute | solution.py:18
  (30 other events, 204.6 us)

commit v3 on v2

--- a/solution.py
+++ b/solution.py
@@ -24,29 +24,96 @@
     return (values * normal_cdf, normal_cdf + values * density)
 
 
-def place_kernel(owner_ref, blocks_ref, out_ref, staged, sem):
+def place_kernel(owner_ref, blocks_ref, out_ref, staged, in_sems, out_sems):
+    count = blocks_ref.shape[0]
+
+    def read(i):
+        return pltpu.make_async_copy(blocks_ref.at[i], staged.at[i], in_sems.at[i])
+
+    def write(i):
+        return pltpu.make_async_copy(staged.at[i], out_ref.at[owner_ref[i]], out_sems.at[i])
+
+    def start(i, carry):
+        read(i).start()
+        return carry
+
     def move(i, carry):
-        staged[owner_ref[i]] = blocks_ref[i]
+        read(i).wait()
+        write(i).start()
         return carry
 
-    lax.fori_loop(0, blocks_ref.shape[0], move, 0)
-    copy = pltpu.make_async_copy(staged, out_ref, sem)
-    copy.start()
-    copy.wait()
+    def wait(i, carry):
+        write(i).wait()
+        return carry
+
+    for step in (start, move, wait):
+        lax.fori_loop(0, count, step, 0)
 
 
 def place(owner, blocks):
     return pl.pallas_call(
         place_kernel,
         out_shape=pltpu.HBM(blocks.shape, blocks.dtype),
-        in_specs=[pl.BlockSpec(memory_space=pltpu.SMEM), pl.BlockSpec(memory_space=pltpu.VMEM)],
+        in_specs=[pl.BlockSpec(memory_space=pltpu.SMEM), pl.BlockSpec(memory_space=pltpu.HBM)],
         out_specs=pl.BlockSpec(memory_space=pltpu.HBM),
-        scratch_shapes=[pltpu.VMEM(blocks.shape, blocks.dtype), pltpu.SemaphoreType.DMA],
-        compiler_params=pltpu.CompilerParams(vmem_limit_bytes=12 << 20),
+        scratch_shapes=[
+            pltpu.VMEM(blocks.shape, blocks.dtype),
+            pltpu.SemaphoreType.DMA((blocks.shape[0],)),
+            pltpu.SemaphoreType.DMA((blocks.shape[0],)),
+        ],
+        compiler_params=pltpu.CompilerParams(vmem_limit_bytes=8 << 20),
         cost_estimate=pl.CostEstimate(
             flops=0, transcendentals=0, bytes_accessed=2 * blocks.size * blocks.dtype.itemsize
         ),
     )(owner, blocks)
+
+
+def finish_kernel(target_ref, late_ref, early_ref, derivative_ref, out_ref, chosen):
+    step = pl.program_id(0)
+
+    @pl.when(step == 0)
+    def _():
+        rows = lax.broadcasted_iota(jnp.int32, chosen.shape, 1)
+        chosen[...] = jnp.where(rows == target_ref[...], 1.0, 0.0).astype(jnp.bfloat16)
+
+    def put(arrived):
+        total = wide(arrived[0]) + wide(arrived[1]) + wide(arrived[2]) + wide(arrived[3])
+        grad = narrow(total * derivative_ref[...])
+        out_ref[...] = narrow(dot(chosen[...], grad, ((1,), (0,))))
+
+    last = pl.num_programs(0) - 1
+
+    @pl.when(step < last)
+    def _():
+        put(late_ref[...])
+
+    @pl.when(step == last)
+    def _():
+        put(early_ref[...])
+
+
+def finish(target, late, early, derivative):
+    tokens, width = early.shape[1:]
+    count = late.shape[2] // width
+    return pl.pallas_call(
+        finish_kernel,
+        grid=(count + 1,),
+        out_shape=jax.ShapeDtypeStruct(derivative.shape, jnp.bfloat16),
+        in_specs=[
+            pl.BlockSpec((tokens, 1), lambda j: (0, 0)),
+            pl.BlockSpec((4, tokens, width), lambda j: (0, 0, jnp.minimum(j, count - 1))),
+            pl.BlockSpec((4, tokens, width), lambda j: (0, 0, 0)),
+            pl.BlockSpec((tokens, width), lambda j: (0, j)),
+        ],
+        out_specs=pl.BlockSpec((tokens, width), lambda j: (0, j)),
+        scratch_shapes=[pltpu.VMEM((tokens, tokens), jnp.bfloat16)],
+        compiler_params=pltpu.CompilerParams(vmem_limit_bytes=16 << 20),
+        cost_estimate=pl.CostEstimate(
+            flops=2 * tokens * derivative.size,
+            transcendentals=0,
+            bytes_accessed=2 * (late.size + early.size) + 6 * derivative.size,
+        ),
+    )(target, late, early, pltpu.with_memory_space_constraint(derivative, pltpu.HBM))
 
 
 def hidden_kernel(rows_ref, weights_ref, out_ref):
@@ -221,14 +288,8 @@
     weights = w_out.reshape(4, 5, units // 5, quarter)
     rows, weights, lhs, derivative = lax.optimization_barrier((rows, weights, lhs, derivative))
 
-    cut = units * 4 // 5
-
     def exchange(terms):
         return lax.all_to_all(terms, "y", split_axis=0, concat_axis=0, tiled=True)
-
-    def hidden_rest(arrived, start, stop):
-        grad = narrow(wide(arrived).sum(axis=0) * derivative[:, start:stop])
-        return narrow(dot(chosen, grad, ((1,), (0,))))
 
     early = hidden_terms(rows, weights, 4, 1)
 
@@ -249,8 +310,7 @@
     sums = [scatter_second(t, second, near) for t, (_, second, near) in zip(totals, PLANS)]
     factor = 1.0 / math.sqrt(owners_total * stripe)
     weight_grad = narrow(jnp.concatenate(sums, axis=1) * factor)
-    parts = [hidden_rest(late, 0, cut), hidden_rest(early, cut, units)]
-    pre_grad = jnp.concatenate(parts, axis=1)
+    pre_grad = finish(target[:, None], late, early, derivative)
     return (pre_grad, weight_grad)
 
 

time: 194 us -> 194 us (level)
  Pallas kernels: 32.3 us -> 38.9 us
  other arithmetic: 20.6 us -> 16.1 us
  matrix products: 23.6 us -> 21.4 us
    pallas_call x0 -> x1, Pallas kernels: none -> 6.25 us  [finish(): pl.pallas_call(finish_kernel, grid=(count + 1,), out_shape=jax.ShapeDtype...]
    reduce_sum x2 -> x0, other arithmetic: 3.7 us -> none  [hidden_rest(): grad = narrow(wide(arrived).sum(axis=0) * derivative[:, start:stop])]
    dot_general x11 -> x9, matrix products: 23.6 us -> 21.4 us  [dot(): lax.dot_general(lhs, rhs, (dims, ((), ())), preferred_element_type=jnp.fl...]
    unnamed x53, local copies, waits for them, and re-layouts: 3.37 us -> 1.17 us
  transfers between devices with their start and end apart: 28 -> 28, of which waited for: 16 -> 14; matrix products, arithmetic and copies ran while one was open for 20% -> 19% of each run, Pallas kernels for 15% -> 15%
where the time goes in v3:
time: 194 us; the launch traced here: 193 us
  waiting for transfers between devices  55.1 us (28%)
  starting transfers between devices  54.1 us (28%)
  Pallas kernels  38.9 us (20%)
  matrix products  21.4 us (11%)
  other arithmetic  16.1 us (8%)
  local copies, waits for them, and re-layouts  5.62 us (3%)
    ppermute x24, waiting for transfers between devices, flip(): return lax.ppermute(value, axis, [(i, i ^ mask) for i in range(size)])  49.7 us
    ppermute x24, starting transfers between devices, flip(): return lax.ppermute(value, axis, [(i, i ^ mask) for i in range(size)])  29.5 us
    dot_general x9, matrix products, dot(): lax.dot_general(lhs, rhs, (dims, ((), ())), preferred_element_type=jnp.fl...  21.4 us
    pallas_call x2, Pallas kernels, hidden_terms(): pl.pallas_call(hidden_kernel, grid=(4,), out_shape=pltpu.HBM((4, tokens,...  18.7 us
    all_to_all x2, starting transfers between devices, exchange(): return lax.all_to_all(terms, 'y', split_axis=0, concat_axis=0, tiled=True)  12.1 us
    convert_element_type x13, other arithmetic, narrow(): return value.astype(jnp.bfloat16)  11.6 us
    pallas_call x2, Pallas kernels, arrange(): pl.pallas_call(functools.partial(arrange_kernel, starts), grid_spec=pltpu...  10.5 us
    all_to_all x1, starting transfers between devices, local(): lax.all_to_all(grad_rows.reshape(owners_total, piece, quarter), SEQ, spli...  8.43 us
  transfers between devices with their start and end apart: 28, of which 14 were waited for; matrix products, arithmetic and copies ran while one was open for 19% of the time, Pallas kernels for 15%

profile of v3, /device:TPU:8, one launch (start us, length us, event | category | flops | bytes accessed | tf_op | source)
XLA Modules:
  0.0 192.5 jit_solution(9316577617911027344)
XLA Ops:
  0.7 8.4 %all-to-all-start = ((bf16[32,16,2048]{2,1,0:T(8,128)(2,1)}), bf16[32,16,2048]{2,1,0:T(8,128)(2,1)}, u32[]{:S(2)}, u32[]{:S(2)}) async-start(bf16[32,16,2048]{2,1,0:T(8,128)(2,1)} %bitcast.161), calls=%async_computation | async-start | bytes 4194304 | tf_op jit(solution)/shard_map/all_to_all | solution.py:254
  19.4 13.7 %collective-permute-done.1.refs_1_ = bf16[2,160,1024]{2,1,0:T(8,128)(2,1)S(1)} collective-permute-done((bf16[2,160,1024]{2,1,0:T(8,128)(2,1)S(1)}, bf16[2,160,1024]{2,1,0:T(8,128)(2,1)S(1)}, u32[]{:S(2)}, u32[]{:S(2)}) %collective-permute-start.1) | collective-permute-done | bytes 655392 | tf_op jit(solution)/shard_map/ppermute | solution.py:18
  34.2 4.9 %all-to-all-done.blocks_ref = bf16[32,16,2048]{2,1,0:T(8,128)(2,1)} async-done(((bf16[32,16,2048]{2,1,0:T(8,128)(2,1)}), bf16[32,16,2048]{2,1,0:T(8,128)(2,1)}, u32[]{:S(2)}, u32[]{:S(2)}) %all-to-all-start) | async-done | bytes 2097184 | tf_op jit(solution)/shard_map/all_to_all | solution.py:254
  39.1 3.4 %shard_map.77 = bf16[32,16,2048]{2,1,0:T(8,128)(2,1)} custom-call(s32[32]{0:T(128)S(1)} %dynamic-slice_reduce_fusion.owner_ref, bf16[32,16,2048]{2,1,0:T(8,128)(2,1)} %all-to-all-done.blocks_ref), custom_call_target="tpu_custom_call" | custom-call | bytes 4194304 | tf_op jit(solution)/shard_map/pallas_call | solution.py:54
  42.5 4.0 %all-to-all-start.1 = ((bf16[32,16,2048]{2,1,0:T(8,128)(2,1)}), bf16[32,16,2048]{2,1,0:T(8,128)(2,1)S(1)}, u32[]{:S(2)}, u32[]{:S(2)}) async-start(bf16[32,16,2048]{2,1,0:T(8,128)(2,1)} %shard_map.77), calls=%async_computation.1 | async-start | bytes 4194304 | tf_op jit(solution)/shard_map/all_to_all | solution.py:286
  51.9 3.5 %fusion.3.derivative_ref = f32[512,1280]{1,0:T(8,128)} fusion(f32[512,1280]{1,0:T(8,128)} %get-tuple-element.75), kind=kLoop, calls=%fused_computation.12 | loop fusion | flops 5242880 | bytes 5242880 | tf_op jit(solution)/shard_map/add | solution.py:24
  55.4 9.0 %collective-permute-done.5.refs_2_ = bf16[2,160,1024]{2,1,0:T(8,128)(2,1)S(1)} collective-permute-done((bf16[2,160,1024]{2,1,0:T(8,128)(2,1)}, bf16[2,160,1024]{2,1,0:T(8,128)(2,1)S(1)}, u32[]{:S(2)}, u32[]{:S(2)}) %collective-permute-start.5) | collective-permute-done | bytes 655392 | tf_op jit(solution)/shard_map/ppermute | solution.py:18
  65.3 7.8 %shard_map.78 = (bf16[16,160,1024]{2,1,0:T(8,128)(2,1)}, bf16[16,160,1024]{2,1,0:T(8,128)(2,1)}, bf16[16,160,1024]{2,1,0:T(8,128)(2,1)}, bf16[16,160,1024]{2,1,0:T(8,128)(2,1)}) custom-call(s32[1]{0:T(128)} %bitcast.14.order_ref, bf16[4,160,1024]{2,1,0:T(8,128)(2,1)S(1)} %pad_maximum_fusion.refs_0_, bf16[2,160,1024]{2,1,0:T(8,128)(2,1)S(1)} %copy-done.3, ...), custom_call_target="tpu_custom_call" | custom-call | bytes 19660800 | tf_op jit(solution)/shard_map/pallas_call | solution.py:207
  73.1 5.5 %collective-permute-done.3.refs_0_ = bf16[2,160,1024]{2,1,0:T(8,128)(2,1)S(1)} collective-permute-done((bf16[2,160,1024]{2,1,0:T(8,128)(2,1)}, bf16[2,160,1024]{2,1,0:T(8,128)(2,1)S(1)}, u32[]{:S(2)}, u32[]{:S(2)}) %collective-permute-start.3) | collective-permute-done | bytes 655392 | tf_op jit(solution)/shard_map/ppermute | solution.py:18
  78.6 2.8 %shard_map.79 = (bf16[16,160,1024]{2,1,0:T(8,128)(2,1)}, bf16[16,160,1024]{2,1,0:T(8,128)(2,1)}, bf16[16,160,1024]{2,1,0:T(8,128)(2,1)}, bf16[16,160,1024]{2,1,0:T(8,128)(2,1)}) custom-call(s32[1]{0:T(128)} %bitcast.14.order_ref, ...), custom_call_target="tpu_custom_call", output_to_operand_aliasing={{0}: (3, {}), {1}: (4, {}), {2}: (5, {}), {3}: (6, {})} | custom-call | bytes 6553600 | tf_op jit(solution)/shard_map/pallas_call | solution.py:207
  81.8 5.8 %shard_map.81 = bf16[4,512,256]{2,1,0:T(8,128)(2,1)} custom-call(bf16[512,2048]{1,0:T(8,128)(2,1)S(1)} %bitcast.125, bf16[4,5,256,2048]{3,2,1,0:T(8,128)(2,1)} %bitcast.128), custom_call_target="tpu_custom_call" | custom-call | flops 2147483648 | bytes 7340032 | tf_op jit(solution)/shard_map/pallas_call | solution.py:127
  89.6 2.6 %convolution_convert_fusion.7 = bf16[1280,512]{1,0:T(8,128)(2,1)} fusion(bf16[2560,1024]{1,0:T(8,128)(2,1)S(1)} %bitcast.134, bf16[1024,2048]{1,0:T(8,128)(2,1)S(1)} %constant_dynamic-update-slice_fusion), kind=kOutput, calls=%fused_computation.8 | convolution fusion | flops 1342832640 | bytes 4980736 | tf_op jit(solution)/shard_map/dot_general | solution.py:146
  94.0 2.6 %convolution_convert_fusion.6 = bf16[1280,512]{1,0:T(8,128)(2,1)} fusion(bf16[2560,1024]{1,0:T(8,128)(2,1)S(1)} %bitcast.137, bf16[1024,2048]{1,0:T(8,128)(2,1)S(1)} %constant_dynamic-update-slice_fusion), kind=kOutput, calls=%fused_computation.7 | convolution fusion | flops 1342832640 | bytes 4980736 | tf_op jit(solution)/shard_map/dot_general | solution.py:146
  98.1 2.6 %convolution_convert_fusion.5 = bf16[1280,512]{1,0:T(8,128)(2,1)} fusion(bf16[2560,1024]{1,0:T(8,128)(2,1)S(1)} %bitcast.143, bf16[1024,2048]{1,0:T(8,128)(2,1)S(1)} %constant_dynamic-update-slice_fusion), kind=kOutput, calls=%fused_computation.6 | convolution fusion | flops 1342832640 | bytes 4980736 | tf_op jit(solution)/shard_map/dot_general | solution.py:146
  102.8 2.6 %convolution_convert_fusion.4 = bf16[1280,512]{1,0:T(8,128)(2,1)} fusion(bf16[2560,1024]{1,0:T(8,128)(2,1)S(1)} %bitcast.149, bf16[1024,2048]{1,0:T(8,128)(2,1)S(1)} %constant_dynamic-update-slice_fusion), kind=kOutput, calls=%fused_computation.5 | convolution fusion | flops 1342832640 | bytes 4980736 | tf_op jit(solution)/shard_map/dot_general | solution.py:146
  107.5 5.7 %all-to-all-start.3 = ((bf16[4,512,256]{2,1,0:T(8,128)(2,1)}), bf16[4,512,256]{2,1,0:T(8,128)(2,1)S(1)}, u32[]{:S(2)}, u32[]{:S(2)}) async-start(bf16[4,512,256]{2,1,0:T(8,128)(2,1)} %shard_map.81), calls=%async_computation.3 | async-start | bytes 2097152 | tf_op jit(solution)/shard_map/all_to_all | solution.py:292
  113.3 13.0 %shard_map.80 = bf16[4,512,1024]{2,1,0:T(8,128)(2,1)} custom-call(bf16[512,2048]{1,0:T(8,128)(2,1)S(1)} %bitcast.127, bf16[4,5,256,2048]{3,2,1,0:T(8,128)(2,1)} %bitcast.129), custom_call_target="tpu_custom_call" | custom-call | flops 8589934592 | bytes 23068672 | tf_op jit(solution)/shard_map/pallas_call | solution.py:127
  126.7 6.4 %all-to-all-start.2 = ((bf16[4,512,1024]{2,1,0:T(8,128)(2,1)}), bf16[4,512,1024]{2,1,0:T(8,128)(2,1)}, u32[]{:S(2)}, u32[]{:S(2)}) async-start(bf16[4,512,1024]{2,1,0:T(8,128)(2,1)} %shard_map.80), calls=%async_computation.2 | async-start | bytes 8388608 | tf_op jit(solution)/shard_map/all_to_all | solution.py:292
  133.1 3.7 %convolution_convert_fusion.3 = bf16[1280,512]{1,0:T(8,128)(2,1)S(1)} fusion(bf16[2560,1024]{1,0:T(8,128)(2,1)} %bitcast.131, bf16[1024,2048]{1,0:T(8,128)(2,1)} %copy-done.6), kind=kOutput, calls=%fused_computation.4 | convolution fusion | flops 1342832640 | bytes 4980736 | tf_op jit(solution)/shard_map/dot_general | solution.py:146
  150.7 9.6 %collective-permute-done.9 = bf16[4,160,512]{2,1,0:T(8,128)(2,1)S(1)} collective-permute-done((bf16[4,160,512]{2,1,0:T(8,128)(2,1)S(1)}, bf16[4,160,512]{2,1,0:T(8,128)(2,1)S(1)}, u32[]{:S(2)}, u32[]{:S(2)}) %collective-permute-start.9) | collective-permute-done | bytes 655392 | tf_op jit(solution)/shard_map/ppermute | solution.py:18
  165.4 2.9 %collective-permute-start.18 = (bf16[2,160,512]{2,1,0:T(8,128)(2,1)S(1)}, bf16[2,160,512]{2,1,0:T(8,128)(2,1)S(1)}, u32[]{:S(2)}, u32[]{:S(2)}) collective-permute-start(bf16[2,160,512]{2,1,0:T(8,128)(2,1)S(1)} %slice.257), channel_id=1, source_target_pairs={{0,96},{32,64},{64,32},{96,0},{1,97},{33,65},{65,33},{97,1},{2,98}... | collective-permute-start | bytes 983048 | tf_op jit(solution)/shard_map/ppermute | solution.py:18
  176.7 3.1 %collective-permute-done.22 = bf16[2,160,512]{2,1,0:T(8,128)(2,1)S(1)} collective-permute-done((bf16[2,160,512]{2,1,0:T(8,128)(2,1)S(1)}, bf16[2,160,512]{2,1,0:T(8,128)(2,1)S(1)}, u32[]{:S(2)}, u32[]{:S(2)}) %collective-permute-start.22) | collective-permute-done | bytes 327712 | tf_op jit(solution)/shard_map/ppermute | solution.py:18
  182.0 3.2 %collective-permute-done.23 = bf16[160,512]{1,0:T(8,128)(2,1)S(1)} collective-permute-done((bf16[160,512]{1,0:T(8,128)(2,1)S(1)}, bf16[160,512]{1,0:T(8,128)(2,1)S(1)}, u32[]{:S(2)}, u32[]{:S(2)}) %collective-permute-start.23) | collective-permute-done | bytes 163872 | tf_op jit(solution)/shard_map/ppermute | solution.py:18
  186.3 6.3 %shard_map.82 = bf16[512,1280]{1,0:T(8,128)(2,1)} custom-call(s32[512,1]{1,0:T(8,128)S(1)} %fusion.41.target_ref, bf16[4,512,1024]{2,1,0:T(8,128)(2,1)} %all-to-all-done.2.late_ref, bf16[4,512,256]{2,1,0:T(8,128)(2,1)S(1)} %all-to-all-done.3.early_ref, f32[512,1280]{1,0:T(8,128)} %fusion.3.derivative_ref), custom_call_target="tpu_custom_call" | custom-call | flops 671088640 | bytes 9175040 | tf_op jit(solution)/shard_map/pallas_call | solution.py:98
  (148 shorter events, 58.1 us)
Async XLA Ops:
  0.7 38.4 %all-to-all-start = ((bf16[32,16,2048]{2,1,0:T(8,128)(2,1)}), bf16[32,16,2048]{2,1,0:T(8,128)(2,1)}, u32[]{:S(2)}, u32[]{:S(2)}) async-start(bf16[32,16,2048]{2,1,0:T(8,128)(2,1)} %bitcast.161), calls=%async_computation | async-start | bytes 4194304 | tf_op jit(solution)/shard_map/all_to_all | solution.py:254
  16.3 16.8 %collective-permute-start.1 = (bf16[2,160,1024]{2,1,0:T(8,128)(2,1)S(1)}, bf16[2,160,1024]{2,1,0:T(8,128)(2,1)S(1)}, u32[]{:S(2)}, u32[]{:S(2)}) collective-permute-start(bf16[2,160,1024]{2,1,0:T(8,128)(2,1)S(1)} %get-tuple-element.33), channel_id=1, source_target_pairs={{0,1},{1,0},{2,3},{3,2},{4,5},{5,4},{6,7},{7,6},{8,9},{9,8},{10,11... | collective-permute-start | bytes 1966088 | tf_op jit(solution)/shard_map/ppermute | solution.py:18
  16.7 17.4 %collective-permute-start.2 = (bf16[2,160,1024]{2,1,0:T(8,128)(2,1)}, bf16[2,160,1024]{2,1,0:T(8,128)(2,1)S(1)}, u32[]{:S(2)}, u32[]{:S(2)}) collective-permute-start(bf16[2,160,1024]{2,1,0:T(8,128)(2,1)} %get-tuple-element.32), channel_id=1, source_target_pairs={{0,3},{1,2},{2,1},{3,0},{4,7},{5,6},{6,5},{7,4},{8,11},{9,10},{10,... | collective-permute-start | bytes 1966088 | tf_op jit(solution)/shard_map/ppermute | solution.py:18
  42.5 38.8 %all-to-all-start.1 = ((bf16[32,16,2048]{2,1,0:T(8,128)(2,1)}), bf16[32,16,2048]{2,1,0:T(8,128)(2,1)S(1)}, u32[]{:S(2)}, u32[]{:S(2)}) async-start(bf16[32,16,2048]{2,1,0:T(8,128)(2,1)} %shard_map.77), calls=%async_computation.1 | async-start | bytes 4194304 | tf_op jit(solution)/shard_map/all_to_all | solution.py:286
  46.6 17.9 %collective-permute-start.5 = (bf16[2,160,1024]{2,1,0:T(8,128)(2,1)}, bf16[2,160,1024]{2,1,0:T(8,128)(2,1)S(1)}, u32[]{:S(2)}, u32[]{:S(2)}) collective-permute-start(bf16[2,160,1024]{2,1,0:T(8,128)(2,1)} %get-tuple-element.32), channel_id=1, source_target_pairs={{0,1},{1,0},{2,3},{3,2},{4,5},{5,4},{6,7},{7,6},{8,9},{9,8},{10,11... | collective-permute-start | bytes 1966088 | tf_op jit(solution)/shard_map/ppermute | solution.py:18
  47.1 18.2 %collective-permute-start.6 = (bf16[2,160,1024]{2,1,0:T(8,128)(2,1)}, bf16[2,160,1024]{2,1,0:T(8,128)(2,1)S(1)}, u32[]{:S(2)}, u32[]{:S(2)}) collective-permute-start(bf16[2,160,1024]{2,1,0:T(8,128)(2,1)} %copy-done.8), channel_id=1, source_target_pairs={{0,3},{1,2},{2,1},{3,0},{4,7},{5,6},{6,5},{7,4},{8,11},{9,10},{10,... | collective-permute-start | bytes 1966088 | tf_op jit(solution)/shard_map/ppermute | solution.py:18
  49.5 29.0 %collective-permute-start.3 = (bf16[2,160,1024]{2,1,0:T(8,128)(2,1)}, bf16[2,160,1024]{2,1,0:T(8,128)(2,1)S(1)}, u32[]{:S(2)}, u32[]{:S(2)}) collective-permute-start(bf16[2,160,1024]{2,1,0:T(8,128)(2,1)} %copy-done.2), channel_id=1, source_target_pairs={{0,3},{1,2},{2,1},{3,0},{4,7},{5,6},{6,5},{7,4},{8,11},{9,10},{10,... | collective-permute-start | bytes 1966088 | tf_op jit(solution)/shard_map/ppermute | solution.py:18
  49.6 29.0 %collective-permute-start.4 = (bf16[2,160,1024]{2,1,0:T(8,128)(2,1)}, bf16[2,160,1024]{2,1,0:T(8,128)(2,1)S(1)}, u32[]{:S(2)}, u32[]{:S(2)}) collective-permute-start(bf16[2,160,1024]{2,1,0:T(8,128)(2,1)} %copy-done.4), channel_id=1, source_target_pairs={{0,1},{1,0},{2,3},{3,2},{4,5},{5,4},{6,7},{7,6},{8,9},{9,8},{10,11... | collective-permute-start | bytes 1966088 | tf_op jit(solution)/shard_map/ppermute | solution.py:18
  92.3 50.6 %collective-permute-start.8 = (bf16[2,4,160,512]{3,2,1,0:T(8,128)(2,1)}, bf16[2,4,160,512]{3,2,1,0:T(8,128)(2,1)}, u32[]{:S(2)}, u32[]{:S(2)}) collective-permute-start(bf16[2,4,160,512]{3,2,1,0:T(8,128)(2,1)} %bitcast.19), channel_id=1, source_target_pairs={{0,8},{8,0},{16,24},{24,16},{1,9},{9,1},{17,25},{25,17},{2,10},{10... | collective-permute-start | bytes 3932168 | tf_op jit(solution)/shard_map/ppermute | solution.py:18
  96.6 48.8 %collective-permute-start.12 = (bf16[2,4,160,512]{3,2,1,0:T(8,128)(2,1)}, bf16[2,4,160,512]{3,2,1,0:T(8,128)(2,1)}, u32[]{:S(2)}, u32[]{:S(2)}) collective-permute-start(bf16[2,4,160,512]{3,2,1,0:T(8,128)(2,1)} %bitcast.21), channel_id=1, source_target_pairs={{0,32},{32,0},{64,96},{96,64},{1,33},{33,1},{65,97},{97,65},{2,34}... | collective-permute-start | bytes 3932168 | tf_op jit(solution)/shard_map/ppermute | solution.py:18
  100.7 47.0 %collective-permute-start.16 = (bf16[2,4,160,512]{3,2,1,0:T(8,128)(2,1)}, bf16[2,4,160,512]{3,2,1,0:T(8,128)(2,1)}, u32[]{:S(2)}, u32[]{:S(2)}) collective-permute-start(bf16[2,4,160,512]{3,2,1,0:T(8,128)(2,1)} %bitcast.23), channel_id=1, source_target_pairs={{0,24},{8,16},{16,8},{24,0},{1,25},{9,17},{17,9},{25,1},{2,26},{10... | collective-permute-start | bytes 3932168 | tf_op jit(solution)/shard_map/ppermute | solution.py:18
  105.4 43.9 %collective-permute-start.20 = (bf16[2,4,160,512]{3,2,1,0:T(8,128)(2,1)}, bf16[2,4,160,512]{3,2,1,0:T(8,128)(2,1)}, u32[]{:S(2)}, u32[]{:S(2)}) collective-permute-start(bf16[2,4,160,512]{3,2,1,0:T(8,128)(2,1)} %bitcast.25), channel_id=1, source_target_pairs={{0,96},{32,64},{64,32},{96,0},{1,97},{33,65},{65,33},{97,1},{2,98}... | collective-permute-start | bytes 3932168 | tf_op jit(solution)/shard_map/ppermute | solution.py:18
  107.5 19.2 %all-to-all-start.3 = ((bf16[4,512,256]{2,1,0:T(8,128)(2,1)}), bf16[4,512,256]{2,1,0:T(8,128)(2,1)S(1)}, u32[]{:S(2)}, u32[]{:S(2)}) async-start(bf16[4,512,256]{2,1,0:T(8,128)(2,1)} %shard_map.81), calls=%async_computation.3 | async-start | bytes 2097152 | tf_op jit(solution)/shard_map/all_to_all | solution.py:292
  126.7 59.5 %all-to-all-start.2 = ((bf16[4,512,1024]{2,1,0:T(8,128)(2,1)}), bf16[4,512,1024]{2,1,0:T(8,128)(2,1)}, u32[]{:S(2)}, u32[]{:S(2)}) async-start(bf16[4,512,1024]{2,1,0:T(8,128)(2,1)} %shard_map.80), calls=%async_computation.2 | async-start | bytes 8388608 | tf_op jit(solution)/shard_map/all_to_all | solution.py:292
  144.1 16.1 %collective-permute-start.9 = (bf16[4,160,512]{2,1,0:T(8,128)(2,1)S(1)}, bf16[4,160,512]{2,1,0:T(8,128)(2,1)S(1)}, u32[]{:S(2)}, u32[]{:S(2)}) collective-permute-start(bf16[4,160,512]{2,1,0:T(8,128)(2,1)S(1)} %fusion.26), channel_id=1, source_target_pairs={{0,24},{8,16},{16,8},{24,0},{1,25},{9,17},{17,9},{25,1},{2,26},{10... | collective-permute-start | bytes 1966088 | tf_op jit(solution)/shard_map/ppermute | solution.py:18
  146.7 15.8 %collective-permute-start.13 = (bf16[4,160,512]{2,1,0:T(8,128)(2,1)S(1)}, bf16[4,160,512]{2,1,0:T(8,128)(2,1)S(1)}, u32[]{:S(2)}, u32[]{:S(2)}) collective-permute-start(bf16[4,160,512]{2,1,0:T(8,128)(2,1)S(1)} %fusion.23), channel_id=1, source_target_pairs={{0,96},{32,64},{64,32},{96,0},{1,97},{33,65},{65,33},{97,1},{2,98}... | collective-permute-start | bytes 1966088 | tf_op jit(solution)/shard_map/ppermute | solution.py:18
  149.0 15.0 %collective-permute-start.17 = (bf16[4,160,512]{2,1,0:T(8,128)(2,1)S(1)}, bf16[4,160,512]{2,1,0:T(8,128)(2,1)S(1)}, u32[]{:S(2)}, u32[]{:S(2)}) collective-permute-start(bf16[4,160,512]{2,1,0:T(8,128)(2,1)S(1)} %fusion.20), channel_id=1, source_target_pairs={{0,8},{8,0},{16,24},{24,16},{1,9},{9,1},{17,25},{25,17},{2,10},{10... | collective-permute-start | bytes 1966088 | tf_op jit(solution)/shard_map/ppermute | solution.py:18
  150.6 17.7 %collective-permute-start.21 = (bf16[4,160,512]{2,1,0:T(8,128)(2,1)S(1)}, bf16[4,160,512]{2,1,0:T(8,128)(2,1)S(1)}, u32[]{:S(2)}, u32[]{:S(2)}) collective-permute-start(bf16[4,160,512]{2,1,0:T(8,128)(2,1)S(1)} %fusion.17), channel_id=1, source_target_pairs={{0,32},{32,0},{64,96},{96,64},{1,33},{33,1},{65,97},{97,65},{2,34}... | collective-permute-start | bytes 1966088 | tf_op jit(solution)/shard_map/ppermute | solution.py:18
  161.6 10.6 %collective-permute-start.10 = (bf16[2,160,512]{2,1,0:T(8,128)(2,1)S(1)}, bf16[2,160,512]{2,1,0:T(8,128)(2,1)S(1)}, u32[]{:S(2)}, u32[]{:S(2)}) collective-permute-start(bf16[2,160,512]{2,1,0:T(8,128)(2,1)S(1)} %slice.239), channel_id=1, source_target_pairs={{0,32},{32,0},{64,96},{96,64},{1,33},{33,1},{65,97},{97,65},{2,34}... | collective-permute-start | bytes 983048 | tf_op jit(solution)/shard_map/ppermute | solution.py:18
  163.9 10.5 %collective-permute-start.14 = (bf16[2,160,512]{2,1,0:T(8,128)(2,1)S(1)}, bf16[2,160,512]{2,1,0:T(8,128)(2,1)S(1)}, u32[]{:S(2)}, u32[]{:S(2)}) collective-permute-start(bf16[2,160,512]{2,1,0:T(8,128)(2,1)S(1)} %slice.248), channel_id=1, source_target_pairs={{0,8},{8,0},{16,24},{24,16},{1,9},{9,1},{17,25},{25,17},{2,10},{10... | collective-permute-start | bytes 983048 | tf_op jit(solution)/shard_map/ppermute | solution.py:18
  165.4 11.2 %collective-permute-start.18 = (bf16[2,160,512]{2,1,0:T(8,128)(2,1)S(1)}, bf16[2,160,512]{2,1,0:T(8,128)(2,1)S(1)}, u32[]{:S(2)}, u32[]{:S(2)}) collective-permute-start(bf16[2,160,512]{2,1,0:T(8,128)(2,1)S(1)} %slice.257), channel_id=1, source_target_pairs={{0,96},{32,64},{64,32},{96,0},{1,97},{33,65},{65,33},{97,1},{2,98}... | collective-permute-start | bytes 983048 | tf_op jit(solution)/shard_map/ppermute | solution.py:18
  169.7 10.1 %collective-permute-start.22 = (bf16[2,160,512]{2,1,0:T(8,128)(2,1)S(1)}, bf16[2,160,512]{2,1,0:T(8,128)(2,1)S(1)}, u32[]{:S(2)}, u32[]{:S(2)}) collective-permute-start(bf16[2,160,512]{2,1,0:T(8,128)(2,1)S(1)} %slice.266), channel_id=1, source_target_pairs={{0,24},{8,16},{16,8},{24,0},{1,25},{9,17},{17,9},{25,1},{2,26},{10... | collective-permute-start | bytes 983048 | tf_op jit(solution)/shard_map/ppermute | solution.py:18
  172.3 8.1 %collective-permute-start.11 = (bf16[160,512]{1,0:T(8,128)(2,1)S(1)}, bf16[160,512]{1,0:T(8,128)(2,1)S(1)}, u32[]{:S(2)}, u32[]{:S(2)}) collective-permute-start(bf16[160,512]{1,0:T(8,128)(2,1)S(1)} %fusion.47), channel_id=1, source_target_pairs={{0,96},{32,64},{64,32},{96,0},{1,97},{33,65},{65,33},{97,1},{2,98}... | collective-permute-start | bytes 491528 | tf_op jit(solution)/shard_map/ppermute | solution.py:18
  174.4 7.2 %collective-permute-start.15 = (bf16[160,512]{1,0:T(8,128)(2,1)S(1)}, bf16[160,512]{1,0:T(8,128)(2,1)S(1)}, u32[]{:S(2)}, u32[]{:S(2)}) collective-permute-start(bf16[160,512]{1,0:T(8,128)(2,1)S(1)} %fusion.48), channel_id=1, source_target_pairs={{0,24},{8,16},{16,8},{24,0},{1,25},{9,17},{17,9},{25,1},{2,26},{10... | collective-permute-start | bytes 491528 | tf_op jit(solution)/shard_map/ppermute | solution.py:18
  (30 other events, 226.5 us)

commit v4 on v3

--- a/solution.py
+++ b/solution.py
@@ -68,45 +68,37 @@
     )(owner, blocks)
 
 
-def finish_kernel(target_ref, late_ref, early_ref, derivative_ref, out_ref, chosen):
-    step = pl.program_id(0)
-
-    @pl.when(step == 0)
-    def _():
-        rows = lax.broadcasted_iota(jnp.int32, chosen.shape, 1)
-        chosen[...] = jnp.where(rows == target_ref[...], 1.0, 0.0).astype(jnp.bfloat16)
-
-    def put(arrived):
-        total = wide(arrived[0]) + wide(arrived[1]) + wide(arrived[2]) + wide(arrived[3])
-        grad = narrow(total * derivative_ref[...])
-        out_ref[...] = narrow(dot(chosen[...], grad, ((1,), (0,))))
-
-    last = pl.num_programs(0) - 1
-
-    @pl.when(step < last)
-    def _():
-        put(late_ref[...])
-
-    @pl.when(step == last)
-    def _():
-        put(early_ref[...])
+def finish_kernel(target_ref, late_ref, early_ref, derivative_ref, out_ref):
+    count = target_ref.shape[0]
+    rows = lax.broadcasted_iota(jnp.int32, (count, count), 1) + pl.program_id(0) * count
+    chosen = jnp.where(rows == target_ref[...], 1.0, 0.0).astype(jnp.bfloat16)
+    start = 0
+    for ref in (late_ref, early_ref):
+        stop = start + ref.shape[2]
+        total = wide(ref[0]) + wide(ref[1]) + wide(ref[2]) + wide(ref[3])
+        grad = narrow(total * derivative_ref[:, start:stop])
+        out_ref[:, start:stop] = narrow(dot(chosen, grad, ((1,), (0,))))
+        start = stop
 
 
 def finish(target, late, early, derivative):
-    tokens, width = early.shape[1:]
-    count = late.shape[2] // width
+    tokens, units = derivative.shape
+    rows = 2 * FRAME
+
+    def arrived(part):
+        return pl.BlockSpec((4, rows, part.shape[2]), lambda i: (0, i, 0))
+
     return pl.pallas_call(
         finish_kernel,
-        grid=(count + 1,),
+        grid=(tokens // rows,),
         out_shape=jax.ShapeDtypeStruct(derivative.shape, jnp.bfloat16),
         in_specs=[
-            pl.BlockSpec((tokens, 1), lambda j: (0, 0)),
-            pl.BlockSpec((4, tokens, width), lambda j: (0, 0, jnp.minimum(j, count - 1))),
-            pl.BlockSpec((4, tokens, width), lambda j: (0, 0, 0)),
-            pl.BlockSpec((tokens, width), lambda j: (0, j)),
+            pl.BlockSpec((rows, 1), lambda i: (i, 0)),
+            arrived(late),
+            arrived(early),
+            pl.BlockSpec((rows, units), lambda i: (i, 0)),
         ],
-        out_specs=pl.BlockSpec((tokens, width), lambda j: (0, j)),
-        scratch_shapes=[pltpu.VMEM((tokens, tokens), jnp.bfloat16)],
+        out_specs=pl.BlockSpec((rows, units), lambda i: (i, 0)),
         compiler_params=pltpu.CompilerParams(vmem_limit_bytes=16 << 20),
         cost_estimate=pl.CostEstimate(
             flops=2 * tokens * derivative.size,

time: 194 us -> 192 us (0.990)
  transfers between devices with their start and end apart: 28 -> 28, of which waited for: 14 -> 14; matrix products, arithmetic and copies ran while one was open for 19% -> 20% of each run, Pallas kernels for 15% -> 15%
where the time goes in v4:
time: 192 us; the launch traced here: 191 us
  waiting for transfers between devices  55 us (29%)
  starting transfers between devices  54.2 us (28%)
  Pallas kernels  37.9 us (20%)
  matrix products  21.4 us (11%)
  other arithmetic  16.1 us (8%)
  local copies, waits for them, and re-layouts  5.62 us (3%)
    ppermute x24, waiting for transfers between devices, flip(): return lax.ppermute(value, axis, [(i, i ^ mask) for i in range(size)])  49.6 us
    ppermute x24, starting transfers between devices, flip(): return lax.ppermute(value, axis, [(i, i ^ mask) for i in range(size)])  29.6 us
    dot_general x9, matrix products, dot(): lax.dot_general(lhs, rhs, (dims, ((), ())), preferred_element_type=jnp.fl...  21.4 us
    pallas_call x2, Pallas kernels, hidden_terms(): pl.pallas_call(hidden_kernel, grid=(4,), out_shape=pltpu.HBM((4, tokens,...  18.7 us
    all_to_all x2, starting transfers between devices, exchange(): return lax.all_to_all(terms, 'y', split_axis=0, concat_axis=0, tiled=True)  12.1 us
    convert_element_type x13, other arithmetic, narrow(): return value.astype(jnp.bfloat16)  11.6 us
    pallas_call x2, Pallas kernels, arrange(): pl.pallas_call(functools.partial(arrange_kernel, starts), grid_spec=pltpu...  10.5 us
    all_to_all x1, starting transfers between devices, local(): lax.all_to_all(grad_rows.reshape(owners_total, piece, quarter), SEQ, spli...  8.43 us
  transfers between devices with their start and end apart: 28, of which 14 were waited for; matrix products, arithmetic and copies ran while one was open for 20% of the time, Pallas kernels for 15%

profile of v4, /device:TPU:8, one launch (start us, length us, event | category | flops | bytes accessed | tf_op | source)
XLA Modules:
  0.0 191.4 jit_solution(12448082485642684211)
XLA Ops:
  0.7 8.4 %all-to-all-start = ((bf16[32,16,2048]{2,1,0:T(8,128)(2,1)}), bf16[32,16,2048]{2,1,0:T(8,128)(2,1)}, u32[]{:S(2)}, u32[]{:S(2)}) async-start(bf16[32,16,2048]{2,1,0:T(8,128)(2,1)} %bitcast.161), calls=%async_computation | async-start | bytes 4194304 | tf_op jit(solution)/shard_map/all_to_all | solution.py:246
  19.4 13.7 %collective-permute-done.1.refs_1_ = bf16[2,160,1024]{2,1,0:T(8,128)(2,1)S(1)} collective-permute-done((bf16[2,160,1024]{2,1,0:T(8,128)(2,1)S(1)}, bf16[2,160,1024]{2,1,0:T(8,128)(2,1)S(1)}, u32[]{:S(2)}, u32[]{:S(2)}) %collective-permute-start.1) | collective-permute-done | bytes 655392 | tf_op jit(solution)/shard_map/ppermute | solution.py:18
  34.2 4.9 %all-to-all-done.blocks_ref = bf16[32,16,2048]{2,1,0:T(8,128)(2,1)} async-done(((bf16[32,16,2048]{2,1,0:T(8,128)(2,1)}), bf16[32,16,2048]{2,1,0:T(8,128)(2,1)}, u32[]{:S(2)}, u32[]{:S(2)}) %all-to-all-start) | async-done | bytes 2097184 | tf_op jit(solution)/shard_map/all_to_all | solution.py:246
  39.1 3.4 %shard_map.77 = bf16[32,16,2048]{2,1,0:T(8,128)(2,1)} custom-call(s32[32]{0:T(128)S(1)} %dynamic-slice_reduce_fusion.owner_ref, bf16[32,16,2048]{2,1,0:T(8,128)(2,1)} %all-to-all-done.blocks_ref), custom_call_target="tpu_custom_call" | custom-call | bytes 4194304 | tf_op jit(solution)/shard_map/pallas_call | solution.py:54
  42.5 4.0 %all-to-all-start.1 = ((bf16[32,16,2048]{2,1,0:T(8,128)(2,1)}), bf16[32,16,2048]{2,1,0:T(8,128)(2,1)S(1)}, u32[]{:S(2)}, u32[]{:S(2)}) async-start(bf16[32,16,2048]{2,1,0:T(8,128)(2,1)} %shard_map.77), calls=%async_computation.1 | async-start | bytes 4194304 | tf_op jit(solution)/shard_map/all_to_all | solution.py:278
  51.9 3.5 %fusion.3.derivative_ref = f32[512,1280]{1,0:T(8,128)} fusion(f32[512,1280]{1,0:T(8,128)} %get-tuple-element.75), kind=kLoop, calls=%fused_computation.12 | loop fusion | flops 5242880 | bytes 5242880 | tf_op jit(solution)/shard_map/add | solution.py:24
  55.4 9.0 %collective-permute-done.5.refs_2_ = bf16[2,160,1024]{2,1,0:T(8,128)(2,1)S(1)} collective-permute-done((bf16[2,160,1024]{2,1,0:T(8,128)(2,1)}, bf16[2,160,1024]{2,1,0:T(8,128)(2,1)S(1)}, u32[]{:S(2)}, u32[]{:S(2)}) %collective-permute-start.5) | collective-permute-done | bytes 655392 | tf_op jit(solution)/shard_map/ppermute | solution.py:18
  65.3 7.8 %shard_map.78 = (bf16[16,160,1024]{2,1,0:T(8,128)(2,1)}, bf16[16,160,1024]{2,1,0:T(8,128)(2,1)}, bf16[16,160,1024]{2,1,0:T(8,128)(2,1)}, bf16[16,160,1024]{2,1,0:T(8,128)(2,1)}) custom-call(s32[1]{0:T(128)} %bitcast.14.order_ref, bf16[4,160,1024]{2,1,0:T(8,128)(2,1)S(1)} %pad_maximum_fusion.refs_0_, bf16[2,160,1024]{2,1,0:T(8,128)(2,1)S(1)} %copy-done.3, ...), custom_call_target="tpu_custom_call" | custom-call | bytes 19660800 | tf_op jit(solution)/shard_map/pallas_call | solution.py:199
  73.0 5.5 %collective-permute-done.3.refs_0_ = bf16[2,160,1024]{2,1,0:T(8,128)(2,1)S(1)} collective-permute-done((bf16[2,160,1024]{2,1,0:T(8,128)(2,1)}, bf16[2,160,1024]{2,1,0:T(8,128)(2,1)S(1)}, u32[]{:S(2)}, u32[]{:S(2)}) %collective-permute-start.3) | collective-permute-done | bytes 655392 | tf_op jit(solution)/shard_map/ppermute | solution.py:18
  78.5 2.8 %shard_map.79 = (bf16[16,160,1024]{2,1,0:T(8,128)(2,1)}, bf16[16,160,1024]{2,1,0:T(8,128)(2,1)}, bf16[16,160,1024]{2,1,0:T(8,128)(2,1)}, bf16[16,160,1024]{2,1,0:T(8,128)(2,1)}) custom-call(s32[1]{0:T(128)} %bitcast.14.order_ref, ...), custom_call_target="tpu_custom_call", output_to_operand_aliasing={{0}: (3, {}), {1}: (4, {}), {2}: (5, {}), {3}: (6, {})} | custom-call | bytes 6553600 | tf_op jit(solution)/shard_map/pallas_call | solution.py:199
  81.8 5.8 %shard_map.81 = bf16[4,512,256]{2,1,0:T(8,128)(2,1)} custom-call(bf16[512,2048]{1,0:T(8,128)(2,1)S(1)} %bitcast.125, bf16[4,5,256,2048]{3,2,1,0:T(8,128)(2,1)} %bitcast.128), custom_call_target="tpu_custom_call" | custom-call | flops 2147483648 | bytes 7340032 | tf_op jit(solution)/shard_map/pallas_call | solution.py:119
  89.6 2.6 %convolution_convert_fusion.7 = bf16[1280,512]{1,0:T(8,128)(2,1)} fusion(bf16[2560,1024]{1,0:T(8,128)(2,1)S(1)} %bitcast.134, bf16[1024,2048]{1,0:T(8,128)(2,1)S(1)} %constant_dynamic-update-slice_fusion), kind=kOutput, calls=%fused_computation.8 | convolution fusion | flops 1342832640 | bytes 4980736 | tf_op jit(solution)/shard_map/dot_general | solution.py:138
  94.0 2.6 %convolution_convert_fusion.6 = bf16[1280,512]{1,0:T(8,128)(2,1)} fusion(bf16[2560,1024]{1,0:T(8,128)(2,1)S(1)} %bitcast.137, bf16[1024,2048]{1,0:T(8,128)(2,1)S(1)} %constant_dynamic-update-slice_fusion), kind=kOutput, calls=%fused_computation.7 | convolution fusion | flops 1342832640 | bytes 4980736 | tf_op jit(solution)/shard_map/dot_general | solution.py:138
  98.1 2.6 %convolution_convert_fusion.5 = bf16[1280,512]{1,0:T(8,128)(2,1)} fusion(bf16[2560,1024]{1,0:T(8,128)(2,1)S(1)} %bitcast.143, bf16[1024,2048]{1,0:T(8,128)(2,1)S(1)} %constant_dynamic-update-slice_fusion), kind=kOutput, calls=%fused_computation.6 | convolution fusion | flops 1342832640 | bytes 4980736 | tf_op jit(solution)/shard_map/dot_general | solution.py:138
  102.8 2.6 %convolution_convert_fusion.4 = bf16[1280,512]{1,0:T(8,128)(2,1)} fusion(bf16[2560,1024]{1,0:T(8,128)(2,1)S(1)} %bitcast.149, bf16[1024,2048]{1,0:T(8,128)(2,1)S(1)} %constant_dynamic-update-slice_fusion), kind=kOutput, calls=%fused_computation.5 | convolution fusion | flops 1342832640 | bytes 4980736 | tf_op jit(solution)/shard_map/dot_general | solution.py:138
  107.5 5.7 %all-to-all-start.3 = ((bf16[4,512,256]{2,1,0:T(8,128)(2,1)}), bf16[4,512,256]{2,1,0:T(8,128)(2,1)S(1)}, u32[]{:S(2)}, u32[]{:S(2)}) async-start(bf16[4,512,256]{2,1,0:T(8,128)(2,1)} %shard_map.81), calls=%async_computation.3 | async-start | bytes 2097152 | tf_op jit(solution)/shard_map/all_to_all | solution.py:284
  113.2 13.0 %shard_map.80 = bf16[4,512,1024]{2,1,0:T(8,128)(2,1)} custom-call(bf16[512,2048]{1,0:T(8,128)(2,1)S(1)} %bitcast.127, bf16[4,5,256,2048]{3,2,1,0:T(8,128)(2,1)} %bitcast.129), custom_call_target="tpu_custom_call" | custom-call | flops 8589934592 | bytes 23068672 | tf_op jit(solution)/shard_map/pallas_call | solution.py:119
  126.7 6.4 %all-to-all-start.2 = ((bf16[4,512,1024]{2,1,0:T(8,128)(2,1)}), bf16[4,512,1024]{2,1,0:T(8,128)(2,1)}, u32[]{:S(2)}, u32[]{:S(2)}) async-start(bf16[4,512,1024]{2,1,0:T(8,128)(2,1)} %shard_map.80), calls=%async_computation.2 | async-start | bytes 8388608 | tf_op jit(solution)/shard_map/all_to_all | solution.py:284
  133.1 3.7 %convolution_convert_fusion.3 = bf16[1280,512]{1,0:T(8,128)(2,1)S(1)} fusion(bf16[2560,1024]{1,0:T(8,128)(2,1)} %bitcast.131, bf16[1024,2048]{1,0:T(8,128)(2,1)} %copy-done.6), kind=kOutput, calls=%fused_computation.4 | convolution fusion | flops 1342832640 | bytes 4980736 | tf_op jit(solution)/shard_map/dot_general | solution.py:138
  150.7 9.6 %collective-permute-done.9 = bf16[4,160,512]{2,1,0:T(8,128)(2,1)S(1)} collective-permute-done((bf16[4,160,512]{2,1,0:T(8,128)(2,1)S(1)}, bf16[4,160,512]{2,1,0:T(8,128)(2,1)S(1)}, u32[]{:S(2)}, u32[]{:S(2)}) %collective-permute-start.9) | collective-permute-done | bytes 655392 | tf_op jit(solution)/shard_map/ppermute | solution.py:18
  165.4 2.8 %collective-permute-start.18 = (bf16[2,160,512]{2,1,0:T(8,128)(2,1)S(1)}, bf16[2,160,512]{2,1,0:T(8,128)(2,1)S(1)}, u32[]{:S(2)}, u32[]{:S(2)}) collective-permute-start(bf16[2,160,512]{2,1,0:T(8,128)(2,1)S(1)} %slice.257), channel_id=1, source_target_pairs={{0,96},{32,64},{64,32},{96,0},{1,97},{33,65},{65,33},{97,1},{2,98}... | collective-permute-start | bytes 983048 | tf_op jit(solution)/shard_map/ppermute | solution.py:18
  176.7 3.1 %collective-permute-done.22 = bf16[2,160,512]{2,1,0:T(8,128)(2,1)S(1)} collective-permute-done((bf16[2,160,512]{2,1,0:T(8,128)(2,1)S(1)}, bf16[2,160,512]{2,1,0:T(8,128)(2,1)S(1)}, u32[]{:S(2)}, u32[]{:S(2)}) %collective-permute-start.22) | collective-permute-done | bytes 327712 | tf_op jit(solution)/shard_map/ppermute | solution.py:18
  182.0 3.1 %collective-permute-done.23 = bf16[160,512]{1,0:T(8,128)(2,1)S(1)} collective-permute-done((bf16[160,512]{1,0:T(8,128)(2,1)S(1)}, bf16[160,512]{1,0:T(8,128)(2,1)S(1)}, u32[]{:S(2)}, u32[]{:S(2)}) %collective-permute-start.23) | collective-permute-done | bytes 163872 | tf_op jit(solution)/shard_map/ppermute | solution.py:18
  186.2 5.2 %shard_map.82 = bf16[512,1280]{1,0:T(8,128)(2,1)} custom-call(s32[512,1]{1,0:T(8,128)S(1)} %fusion.41.target_ref, bf16[4,512,1024]{2,1,0:T(8,128)(2,1)} %all-to-all-done.2.late_ref, bf16[4,512,256]{2,1,0:T(8,128)(2,1)S(1)} %all-to-all-done.3.early_ref, f32[512,1280]{1,0:T(8,128)} %fusion.3.derivative_ref), custom_call_target="tpu_custom_call" | custom-call | flops 671088640 | bytes 9175040 | tf_op jit(solution)/shard_map/pallas_call | solution.py:91
  (148 shorter events, 58.3 us)
Async XLA Ops:
  0.7 38.4 %all-to-all-start = ((bf16[32,16,2048]{2,1,0:T(8,128)(2,1)}), bf16[32,16,2048]{2,1,0:T(8,128)(2,1)}, u32[]{:S(2)}, u32[]{:S(2)}) async-start(bf16[32,16,2048]{2,1,0:T(8,128)(2,1)} %bitcast.161), calls=%async_computation | async-start | bytes 4194304 | tf_op jit(solution)/shard_map/all_to_all | solution.py:246
  16.3 16.8 %collective-permute-start.1 = (bf16[2,160,1024]{2,1,0:T(8,128)(2,1)S(1)}, bf16[2,160,1024]{2,1,0:T(8,128)(2,1)S(1)}, u32[]{:S(2)}, u32[]{:S(2)}) collective-permute-start(bf16[2,160,1024]{2,1,0:T(8,128)(2,1)S(1)} %get-tuple-element.33), channel_id=1, source_target_pairs={{0,1},{1,0},{2,3},{3,2},{4,5},{5,4},{6,7},{7,6},{8,9},{9,8},{10,11... | collective-permute-start | bytes 1966088 | tf_op jit(solution)/shard_map/ppermute | solution.py:18
  16.7 17.4 %collective-permute-start.2 = (bf16[2,160,1024]{2,1,0:T(8,128)(2,1)}, bf16[2,160,1024]{2,1,0:T(8,128)(2,1)S(1)}, u32[]{:S(2)}, u32[]{:S(2)}) collective-permute-start(bf16[2,160,1024]{2,1,0:T(8,128)(2,1)} %get-tuple-element.32), channel_id=1, source_target_pairs={{0,3},{1,2},{2,1},{3,0},{4,7},{5,6},{6,5},{7,4},{8,11},{9,10},{10,... | collective-permute-start | bytes 1966088 | tf_op jit(solution)/shard_map/ppermute | solution.py:18
  42.5 38.8 %all-to-all-start.1 = ((bf16[32,16,2048]{2,1,0:T(8,128)(2,1)}), bf16[32,16,2048]{2,1,0:T(8,128)(2,1)S(1)}, u32[]{:S(2)}, u32[]{:S(2)}) async-start(bf16[32,16,2048]{2,1,0:T(8,128)(2,1)} %shard_map.77), calls=%async_computation.1 | async-start | bytes 4194304 | tf_op jit(solution)/shard_map/all_to_all | solution.py:278
  46.6 17.9 %collective-permute-start.5 = (bf16[2,160,1024]{2,1,0:T(8,128)(2,1)}, bf16[2,160,1024]{2,1,0:T(8,128)(2,1)S(1)}, u32[]{:S(2)}, u32[]{:S(2)}) collective-permute-start(bf16[2,160,1024]{2,1,0:T(8,128)(2,1)} %get-tuple-element.32), channel_id=1, source_target_pairs={{0,1},{1,0},{2,3},{3,2},{4,5},{5,4},{6,7},{7,6},{8,9},{9,8},{10,11... | collective-permute-start | bytes 1966088 | tf_op jit(solution)/shard_map/ppermute | solution.py:18
  47.1 18.2 %collective-permute-start.6 = (bf16[2,160,1024]{2,1,0:T(8,128)(2,1)}, bf16[2,160,1024]{2,1,0:T(8,128)(2,1)S(1)}, u32[]{:S(2)}, u32[]{:S(2)}) collective-permute-start(bf16[2,160,1024]{2,1,0:T(8,128)(2,1)} %copy-done.8), channel_id=1, source_target_pairs={{0,3},{1,2},{2,1},{3,0},{4,7},{5,6},{6,5},{7,4},{8,11},{9,10},{10,... | collective-permute-start | bytes 1966088 | tf_op jit(solution)/shard_map/ppermute | solution.py:18
  49.5 29.0 %collective-permute-start.3 = (bf16[2,160,1024]{2,1,0:T(8,128)(2,1)}, bf16[2,160,1024]{2,1,0:T(8,128)(2,1)S(1)}, u32[]{:S(2)}, u32[]{:S(2)}) collective-permute-start(bf16[2,160,1024]{2,1,0:T(8,128)(2,1)} %copy-done.2), channel_id=1, source_target_pairs={{0,3},{1,2},{2,1},{3,0},{4,7},{5,6},{6,5},{7,4},{8,11},{9,10},{10,... | collective-permute-start | bytes 1966088 | tf_op jit(solution)/shard_map/ppermute | solution.py:18
  49.5 29.0 %collective-permute-start.4 = (bf16[2,160,1024]{2,1,0:T(8,128)(2,1)}, bf16[2,160,1024]{2,1,0:T(8,128)(2,1)S(1)}, u32[]{:S(2)}, u32[]{:S(2)}) collective-permute-start(bf16[2,160,1024]{2,1,0:T(8,128)(2,1)} %copy-done.4), channel_id=1, source_target_pairs={{0,1},{1,0},{2,3},{3,2},{4,5},{5,4},{6,7},{7,6},{8,9},{9,8},{10,11... | collective-permute-start | bytes 1966088 | tf_op jit(solution)/shard_map/ppermute | solution.py:18
  92.3 50.6 %collective-permute-start.8 = (bf16[2,4,160,512]{3,2,1,0:T(8,128)(2,1)}, bf16[2,4,160,512]{3,2,1,0:T(8,128)(2,1)}, u32[]{:S(2)}, u32[]{:S(2)}) collective-permute-start(bf16[2,4,160,512]{3,2,1,0:T(8,128)(2,1)} %bitcast.19), channel_id=1, source_target_pairs={{0,8},{8,0},{16,24},{24,16},{1,9},{9,1},{17,25},{25,17},{2,10},{10... | collective-permute-start | bytes 3932168 | tf_op jit(solution)/shard_map/ppermute | solution.py:18
  96.6 48.8 %collective-permute-start.12 = (bf16[2,4,160,512]{3,2,1,0:T(8,128)(2,1)}, bf16[2,4,160,512]{3,2,1,0:T(8,128)(2,1)}, u32[]{:S(2)}, u32[]{:S(2)}) collective-permute-start(bf16[2,4,160,512]{3,2,1,0:T(8,128)(2,1)} %bitcast.21), channel_id=1, source_target_pairs={{0,32},{32,0},{64,96},{96,64},{1,33},{33,1},{65,97},{97,65},{2,34}... | collective-permute-start | bytes 3932168 | tf_op jit(solution)/shard_map/ppermute | solution.py:18
  100.7 47.0 %collective-permute-start.16 = (bf16[2,4,160,512]{3,2,1,0:T(8,128)(2,1)}, bf16[2,4,160,512]{3,2,1,0:T(8,128)(2,1)}, u32[]{:S(2)}, u32[]{:S(2)}) collective-permute-start(bf16[2,4,160,512]{3,2,1,0:T(8,128)(2,1)} %bitcast.23), channel_id=1, source_target_pairs={{0,24},{8,16},{16,8},{24,0},{1,25},{9,17},{17,9},{25,1},{2,26},{10... | collective-permute-start | bytes 3932168 | tf_op jit(solution)/shard_map/ppermute | solution.py:18
  105.4 43.9 %collective-permute-start.20 = (bf16[2,4,160,512]{3,2,1,0:T(8,128)(2,1)}, bf16[2,4,160,512]{3,2,1,0:T(8,128)(2,1)}, u32[]{:S(2)}, u32[]{:S(2)}) collective-permute-start(bf16[2,4,160,512]{3,2,1,0:T(8,128)(2,1)} %bitcast.25), channel_id=1, source_target_pairs={{0,96},{32,64},{64,32},{96,0},{1,97},{33,65},{65,33},{97,1},{2,98}... | collective-permute-start | bytes 3932168 | tf_op jit(solution)/shard_map/ppermute | solution.py:18
  107.5 19.2 %all-to-all-start.3 = ((bf16[4,512,256]{2,1,0:T(8,128)(2,1)}), bf16[4,512,256]{2,1,0:T(8,128)(2,1)S(1)}, u32[]{:S(2)}, u32[]{:S(2)}) async-start(bf16[4,512,256]{2,1,0:T(8,128)(2,1)} %shard_map.81), calls=%async_computation.3 | async-start | bytes 2097152 | tf_op jit(solution)/shard_map/all_to_all | solution.py:284
  126.7 59.5 %all-to-all-start.2 = ((bf16[4,512,1024]{2,1,0:T(8,128)(2,1)}), bf16[4,512,1024]{2,1,0:T(8,128)(2,1)}, u32[]{:S(2)}, u32[]{:S(2)}) async-start(bf16[4,512,1024]{2,1,0:T(8,128)(2,1)} %shard_map.80), calls=%async_computation.2 | async-start | bytes 8388608 | tf_op jit(solution)/shard_map/all_to_all | solution.py:284
  144.1 16.1 %collective-permute-start.9 = (bf16[4,160,512]{2,1,0:T(8,128)(2,1)S(1)}, bf16[4,160,512]{2,1,0:T(8,128)(2,1)S(1)}, u32[]{:S(2)}, u32[]{:S(2)}) collective-permute-start(bf16[4,160,512]{2,1,0:T(8,128)(2,1)S(1)} %fusion.26), channel_id=1, source_target_pairs={{0,24},{8,16},{16,8},{24,0},{1,25},{9,17},{17,9},{25,1},{2,26},{10... | collective-permute-start | bytes 1966088 | tf_op jit(solution)/shard_map/ppermute | solution.py:18
  146.6 15.8 %collective-permute-start.13 = (bf16[4,160,512]{2,1,0:T(8,128)(2,1)S(1)}, bf16[4,160,512]{2,1,0:T(8,128)(2,1)S(1)}, u32[]{:S(2)}, u32[]{:S(2)}) collective-permute-start(bf16[4,160,512]{2,1,0:T(8,128)(2,1)S(1)} %fusion.23), channel_id=1, source_target_pairs={{0,96},{32,64},{64,32},{96,0},{1,97},{33,65},{65,33},{97,1},{2,98}... | collective-permute-start | bytes 1966088 | tf_op jit(solution)/shard_map/ppermute | solution.py:18
  149.0 15.0 %collective-permute-start.17 = (bf16[4,160,512]{2,1,0:T(8,128)(2,1)S(1)}, bf16[4,160,512]{2,1,0:T(8,128)(2,1)S(1)}, u32[]{:S(2)}, u32[]{:S(2)}) collective-permute-start(bf16[4,160,512]{2,1,0:T(8,128)(2,1)S(1)} %fusion.20), channel_id=1, source_target_pairs={{0,8},{8,0},{16,24},{24,16},{1,9},{9,1},{17,25},{25,17},{2,10},{10... | collective-permute-start | bytes 1966088 | tf_op jit(solution)/shard_map/ppermute | solution.py:18
  150.6 17.6 %collective-permute-start.21 = (bf16[4,160,512]{2,1,0:T(8,128)(2,1)S(1)}, bf16[4,160,512]{2,1,0:T(8,128)(2,1)S(1)}, u32[]{:S(2)}, u32[]{:S(2)}) collective-permute-start(bf16[4,160,512]{2,1,0:T(8,128)(2,1)S(1)} %fusion.17), channel_id=1, source_target_pairs={{0,32},{32,0},{64,96},{96,64},{1,33},{33,1},{65,97},{97,65},{2,34}... | collective-permute-start | bytes 1966088 | tf_op jit(solution)/shard_map/ppermute | solution.py:18
  161.6 10.6 %collective-permute-start.10 = (bf16[2,160,512]{2,1,0:T(8,128)(2,1)S(1)}, bf16[2,160,512]{2,1,0:T(8,128)(2,1)S(1)}, u32[]{:S(2)}, u32[]{:S(2)}) collective-permute-start(bf16[2,160,512]{2,1,0:T(8,128)(2,1)S(1)} %slice.239), channel_id=1, source_target_pairs={{0,32},{32,0},{64,96},{96,64},{1,33},{33,1},{65,97},{97,65},{2,34}... | collective-permute-start | bytes 983048 | tf_op jit(solution)/shard_map/ppermute | solution.py:18
  163.8 10.5 %collective-permute-start.14 = (bf16[2,160,512]{2,1,0:T(8,128)(2,1)S(1)}, bf16[2,160,512]{2,1,0:T(8,128)(2,1)S(1)}, u32[]{:S(2)}, u32[]{:S(2)}) collective-permute-start(bf16[2,160,512]{2,1,0:T(8,128)(2,1)S(1)} %slice.248), channel_id=1, source_target_pairs={{0,8},{8,0},{16,24},{24,16},{1,9},{9,1},{17,25},{25,17},{2,10},{10... | collective-permute-start | bytes 983048 | tf_op jit(solution)/shard_map/ppermute | solution.py:18
  165.4 11.1 %collective-permute-start.18 = (bf16[2,160,512]{2,1,0:T(8,128)(2,1)S(1)}, bf16[2,160,512]{2,1,0:T(8,128)(2,1)S(1)}, u32[]{:S(2)}, u32[]{:S(2)}) collective-permute-start(bf16[2,160,512]{2,1,0:T(8,128)(2,1)S(1)} %slice.257), channel_id=1, source_target_pairs={{0,96},{32,64},{64,32},{96,0},{1,97},{33,65},{65,33},{97,1},{2,98}... | collective-permute-start | bytes 983048 | tf_op jit(solution)/shard_map/ppermute | solution.py:18
  169.6 10.1 %collective-permute-start.22 = (bf16[2,160,512]{2,1,0:T(8,128)(2,1)S(1)}, bf16[2,160,512]{2,1,0:T(8,128)(2,1)S(1)}, u32[]{:S(2)}, u32[]{:S(2)}) collective-permute-start(bf16[2,160,512]{2,1,0:T(8,128)(2,1)S(1)} %slice.266), channel_id=1, source_target_pairs={{0,24},{8,16},{16,8},{24,0},{1,25},{9,17},{17,9},{25,1},{2,26},{10... | collective-permute-start | bytes 983048 | tf_op jit(solution)/shard_map/ppermute | solution.py:18
  172.2 8.1 %collective-permute-start.11 = (bf16[160,512]{1,0:T(8,128)(2,1)S(1)}, bf16[160,512]{1,0:T(8,128)(2,1)S(1)}, u32[]{:S(2)}, u32[]{:S(2)}) collective-permute-start(bf16[160,512]{1,0:T(8,128)(2,1)S(1)} %fusion.47), channel_id=1, source_target_pairs={{0,96},{32,64},{64,32},{96,0},{1,97},{33,65},{65,33},{97,1},{2,98}... | collective-permute-start | bytes 491528 | tf_op jit(solution)/shard_map/ppermute | solution.py:18
  174.3 7.1 %collective-permute-start.15 = (bf16[160,512]{1,0:T(8,128)(2,1)S(1)}, bf16[160,512]{1,0:T(8,128)(2,1)S(1)}, u32[]{:S(2)}, u32[]{:S(2)}) collective-permute-start(bf16[160,512]{1,0:T(8,128)(2,1)S(1)} %fusion.48), channel_id=1, source_target_pairs={{0,24},{8,16},{16,8},{24,0},{1,25},{9,17},{17,9},{25,1},{2,26},{10... | collective-permute-start | bytes 491528 | tf_op jit(solution)/shard_map/ppermute | solution.py:18
  (30 other events, 225.4 us)

commit v5 on v4

--- a/solution.py
+++ b/solution.py
@@ -83,7 +83,7 @@
 
 def finish(target, late, early, derivative):
     tokens, units = derivative.shape
-    rows = 2 * FRAME
+    rows = FRAME
 
     def arrived(part):
         return pl.BlockSpec((4, rows, part.shape[2]), lambda i: (0, i, 0))

time: 192 us -> 195 us (1.016)
  Pallas kernels: 37.9 us -> 39.9 us
    pallas_call x1, Pallas kernels: 5.17 us -> 7.19 us  [finish(): pl.pallas_call(finish_kernel, grid=(tokens // rows,), out_shape=jax.Shape...]
  transfers between devices with their start and end apart: 28 -> 28, of which waited for: 14 -> 14; matrix products, arithmetic and copies ran while one was open for 20% -> 19% of each run, Pallas kernels for 15% -> 15%
where the time goes in v5:
time: 195 us; the launch traced here: 193 us
  waiting for transfers between devices  55.1 us (28%)
  starting transfers between devices  54.1 us (28%)
  Pallas kernels  39.9 us (20%)
  matrix products  21.4 us (11%)
  other arithmetic  16.1 us (8%)
  local copies, waits for them, and re-layouts  5.62 us (3%)
    ppermute x24, waiting for transfers between devices, flip(): return lax.ppermute(value, axis, [(i, i ^ mask) for i in range(size)])  49.7 us
    ppermute x24, starting transfers between devices, flip(): return lax.ppermute(value, axis, [(i, i ^ mask) for i in range(size)])  29.5 us
    dot_general x9, matrix products, dot(): lax.dot_general(lhs, rhs, (dims, ((), ())), preferred_element_type=jnp.fl...  21.4 us
    pallas_call x2, Pallas kernels, hidden_terms(): pl.pallas_call(hidden_kernel, grid=(4,), out_shape=pltpu.HBM((4, tokens,...  18.7 us
    all_to_all x2, starting transfers between devices, exchange(): return lax.all_to_all(terms, 'y', split_axis=0, concat_axis=0, tiled=True)  12.1 us
    convert_element_type x13, other arithmetic, narrow(): return value.astype(jnp.bfloat16)  11.6 us
    pallas_call x2, Pallas kernels, arrange(): pl.pallas_call(functools.partial(arrange_kernel, starts), grid_spec=pltpu...  10.5 us
    all_to_all x1, starting transfers between devices, local(): lax.all_to_all(grad_rows.reshape(owners_total, piece, quarter), SEQ, spli...  8.43 us
  transfers between devices with their start and end apart: 28, of which 14 were waited for; matrix products, arithmetic and copies ran while one was open for 19% of the time, Pallas kernels for 15%

profile of v5, /device:TPU:8, one launch (start us, length us, event | category | flops | bytes accessed | tf_op | source)
XLA Modules:
  0.0 193.4 jit_solution(16064979310151925256)
XLA Ops:
  0.7 8.4 %all-to-all-start = ((bf16[32,16,2048]{2,1,0:T(8,128)(2,1)}), bf16[32,16,2048]{2,1,0:T(8,128)(2,1)}, u32[]{:S(2)}, u32[]{:S(2)}) async-start(bf16[32,16,2048]{2,1,0:T(8,128)(2,1)} %bitcast.161), calls=%async_computation | async-start | bytes 4194304 | tf_op jit(solution)/shard_map/all_to_all | solution.py:246
  19.4 13.7 %collective-permute-done.1.refs_1_ = bf16[2,160,1024]{2,1,0:T(8,128)(2,1)S(1)} collective-permute-done((bf16[2,160,1024]{2,1,0:T(8,128)(2,1)S(1)}, bf16[2,160,1024]{2,1,0:T(8,128)(2,1)S(1)}, u32[]{:S(2)}, u32[]{:S(2)}) %collective-permute-start.1) | collective-permute-done | bytes 655392 | tf_op jit(solution)/shard_map/ppermute | solution.py:18
  34.2 4.9 %all-to-all-done.blocks_ref = bf16[32,16,2048]{2,1,0:T(8,128)(2,1)} async-done(((bf16[32,16,2048]{2,1,0:T(8,128)(2,1)}), bf16[32,16,2048]{2,1,0:T(8,128)(2,1)}, u32[]{:S(2)}, u32[]{:S(2)}) %all-to-all-start) | async-done | bytes 2097184 | tf_op jit(solution)/shard_map/all_to_all | solution.py:246
  39.1 3.4 %shard_map.77 = bf16[32,16,2048]{2,1,0:T(8,128)(2,1)} custom-call(s32[32]{0:T(128)S(1)} %dynamic-slice_reduce_fusion.owner_ref, bf16[32,16,2048]{2,1,0:T(8,128)(2,1)} %all-to-all-done.blocks_ref), custom_call_target="tpu_custom_call" | custom-call | bytes 4194304 | tf_op jit(solution)/shard_map/pallas_call | solution.py:54
  42.5 4.0 %all-to-all-start.1 = ((bf16[32,16,2048]{2,1,0:T(8,128)(2,1)}), bf16[32,16,2048]{2,1,0:T(8,128)(2,1)S(1)}, u32[]{:S(2)}, u32[]{:S(2)}) async-start(bf16[32,16,2048]{2,1,0:T(8,128)(2,1)} %shard_map.77), calls=%async_computation.1 | async-start | bytes 4194304 | tf_op jit(solution)/shard_map/all_to_all | solution.py:278
  51.9 3.5 %fusion.3.derivative_ref = f32[512,1280]{1,0:T(8,128)} fusion(f32[512,1280]{1,0:T(8,128)} %get-tuple-element.75), kind=kLoop, calls=%fused_computation.12 | loop fusion | flops 5242880 | bytes 5242880 | tf_op jit(solution)/shard_map/add | solution.py:24
  55.4 9.0 %collective-permute-done.5.refs_2_ = bf16[2,160,1024]{2,1,0:T(8,128)(2,1)S(1)} collective-permute-done((bf16[2,160,1024]{2,1,0:T(8,128)(2,1)}, bf16[2,160,1024]{2,1,0:T(8,128)(2,1)S(1)}, u32[]{:S(2)}, u32[]{:S(2)}) %collective-permute-start.5) | collective-permute-done | bytes 655392 | tf_op jit(solution)/shard_map/ppermute | solution.py:18
  65.3 7.8 %shard_map.78 = (bf16[16,160,1024]{2,1,0:T(8,128)(2,1)}, bf16[16,160,1024]{2,1,0:T(8,128)(2,1)}, bf16[16,160,1024]{2,1,0:T(8,128)(2,1)}, bf16[16,160,1024]{2,1,0:T(8,128)(2,1)}) custom-call(s32[1]{0:T(128)} %bitcast.14.order_ref, bf16[4,160,1024]{2,1,0:T(8,128)(2,1)S(1)} %pad_maximum_fusion.refs_0_, bf16[2,160,1024]{2,1,0:T(8,128)(2,1)S(1)} %copy-done.3, ...), custom_call_target="tpu_custom_call" | custom-call | bytes 19660800 | tf_op jit(solution)/shard_map/pallas_call | solution.py:199
  73.0 5.5 %collective-permute-done.3.refs_0_ = bf16[2,160,1024]{2,1,0:T(8,128)(2,1)S(1)} collective-permute-done((bf16[2,160,1024]{2,1,0:T(8,128)(2,1)}, bf16[2,160,1024]{2,1,0:T(8,128)(2,1)S(1)}, u32[]{:S(2)}, u32[]{:S(2)}) %collective-permute-start.3) | collective-permute-done | bytes 655392 | tf_op jit(solution)/shard_map/ppermute | solution.py:18
  78.5 2.8 %shard_map.79 = (bf16[16,160,1024]{2,1,0:T(8,128)(2,1)}, bf16[16,160,1024]{2,1,0:T(8,128)(2,1)}, bf16[16,160,1024]{2,1,0:T(8,128)(2,1)}, bf16[16,160,1024]{2,1,0:T(8,128)(2,1)}) custom-call(s32[1]{0:T(128)} %bitcast.14.order_ref, ...), custom_call_target="tpu_custom_call", output_to_operand_aliasing={{0}: (3, {}), {1}: (4, {}), {2}: (5, {}), {3}: (6, {})} | custom-call | bytes 6553600 | tf_op jit(solution)/shard_map/pallas_call | solution.py:199
  81.8 5.8 %shard_map.81 = bf16[4,512,256]{2,1,0:T(8,128)(2,1)} custom-call(bf16[512,2048]{1,0:T(8,128)(2,1)S(1)} %bitcast.125, bf16[4,5,256,2048]{3,2,1,0:T(8,128)(2,1)} %bitcast.128), custom_call_target="tpu_custom_call" | custom-call | flops 2147483648 | bytes 7340032 | tf_op jit(solution)/shard_map/pallas_call | solution.py:119
  89.6 2.6 %convolution_convert_fusion.7 = bf16[1280,512]{1,0:T(8,128)(2,1)} fusion(bf16[2560,1024]{1,0:T(8,128)(2,1)S(1)} %bitcast.134, bf16[1024,2048]{1,0:T(8,128)(2,1)S(1)} %constant_dynamic-update-slice_fusion), kind=kOutput, calls=%fused_computation.8 | convolution fusion | flops 1342832640 | bytes 4980736 | tf_op jit(solution)/shard_map/dot_general | solution.py:138
  93.9 2.6 %convolution_convert_fusion.6 = bf16[1280,512]{1,0:T(8,128)(2,1)} fusion(bf16[2560,1024]{1,0:T(8,128)(2,1)S(1)} %bitcast.137, bf16[1024,2048]{1,0:T(8,128)(2,1)S(1)} %constant_dynamic-update-slice_fusion), kind=kOutput, calls=%fused_computation.7 | convolution fusion | flops 1342832640 | bytes 4980736 | tf_op jit(solution)/shard_map/dot_general | solution.py:138
  98.1 2.6 %convolution_convert_fusion.5 = bf16[1280,512]{1,0:T(8,128)(2,1)} fusion(bf16[2560,1024]{1,0:T(8,128)(2,1)S(1)} %bitcast.143, bf16[1024,2048]{1,0:T(8,128)(2,1)S(1)} %constant_dynamic-update-slice_fusion), kind=kOutput, calls=%fused_computation.6 | convolution fusion | flops 1342832640 | bytes 4980736 | tf_op jit(solution)/shard_map/dot_general | solution.py:138
  102.8 2.6 %convolution_convert_fusion.4 = bf16[1280,512]{1,0:T(8,128)(2,1)} fusion(bf16[2560,1024]{1,0:T(8,128)(2,1)S(1)} %bitcast.149, bf16[1024,2048]{1,0:T(8,128)(2,1)S(1)} %constant_dynamic-update-slice_fusion), kind=kOutput, calls=%fused_computation.5 | convolution fusion | flops 1342832640 | bytes 4980736 | tf_op jit(solution)/shard_map/dot_general | solution.py:138
  107.5 5.7 %all-to-all-start.3 = ((bf16[4,512,256]{2,1,0:T(8,128)(2,1)}), bf16[4,512,256]{2,1,0:T(8,128)(2,1)S(1)}, u32[]{:S(2)}, u32[]{:S(2)}) async-start(bf16[4,512,256]{2,1,0:T(8,128)(2,1)} %shard_map.81), calls=%async_computation.3 | async-start | bytes 2097152 | tf_op jit(solution)/shard_map/all_to_all | solution.py:284
  113.2 13.0 %shard_map.80 = bf16[4,512,1024]{2,1,0:T(8,128)(2,1)} custom-call(bf16[512,2048]{1,0:T(8,128)(2,1)S(1)} %bitcast.127, bf16[4,5,256,2048]{3,2,1,0:T(8,128)(2,1)} %bitcast.129), custom_call_target="tpu_custom_call" | custom-call | flops 8589934592 | bytes 23068672 | tf_op jit(solution)/shard_map/pallas_call | solution.py:119
  126.7 6.4 %all-to-all-start.2 = ((bf16[4,512,1024]{2,1,0:T(8,128)(2,1)}), bf16[4,512,1024]{2,1,0:T(8,128)(2,1)}, u32[]{:S(2)}, u32[]{:S(2)}) async-start(bf16[4,512,1024]{2,1,0:T(8,128)(2,1)} %shard_map.80), calls=%async_computation.2 | async-start | bytes 8388608 | tf_op jit(solution)/shard_map/all_to_all | solution.py:284
  133.1 3.7 %convolution_convert_fusion.3 = bf16[1280,512]{1,0:T(8,128)(2,1)S(1)} fusion(bf16[2560,1024]{1,0:T(8,128)(2,1)} %bitcast.131, bf16[1024,2048]{1,0:T(8,128)(2,1)} %copy-done.6), kind=kOutput, calls=%fused_computation.4 | convolution fusion | flops 1342832640 | bytes 4980736 | tf_op jit(solution)/shard_map/dot_general | solution.py:138
  150.7 9.6 %collective-permute-done.9 = bf16[4,160,512]{2,1,0:T(8,128)(2,1)S(1)} collective-permute-done((bf16[4,160,512]{2,1,0:T(8,128)(2,1)S(1)}, bf16[4,160,512]{2,1,0:T(8,128)(2,1)S(1)}, u32[]{:S(2)}, u32[]{:S(2)}) %collective-permute-start.9) | collective-permute-done | bytes 655392 | tf_op jit(solution)/shard_map/ppermute | solution.py:18
  165.3 2.9 %collective-permute-start.18 = (bf16[2,160,512]{2,1,0:T(8,128)(2,1)S(1)}, bf16[2,160,512]{2,1,0:T(8,128)(2,1)S(1)}, u32[]{:S(2)}, u32[]{:S(2)}) collective-permute-start(bf16[2,160,512]{2,1,0:T(8,128)(2,1)S(1)} %slice.257), channel_id=1, source_target_pairs={{0,96},{32,64},{64,32},{96,0},{1,97},{33,65},{65,33},{97,1},{2,98}... | collective-permute-start | bytes 983048 | tf_op jit(solution)/shard_map/ppermute | solution.py:18
  176.6 3.1 %collective-permute-done.22 = bf16[2,160,512]{2,1,0:T(8,128)(2,1)S(1)} collective-permute-done((bf16[2,160,512]{2,1,0:T(8,128)(2,1)S(1)}, bf16[2,160,512]{2,1,0:T(8,128)(2,1)S(1)}, u32[]{:S(2)}, u32[]{:S(2)}) %collective-permute-start.22) | collective-permute-done | bytes 327712 | tf_op jit(solution)/shard_map/ppermute | solution.py:18
  182.0 3.2 %collective-permute-done.23 = bf16[160,512]{1,0:T(8,128)(2,1)S(1)} collective-permute-done((bf16[160,512]{1,0:T(8,128)(2,1)S(1)}, bf16[160,512]{1,0:T(8,128)(2,1)S(1)}, u32[]{:S(2)}, u32[]{:S(2)}) %collective-permute-start.23) | collective-permute-done | bytes 163872 | tf_op jit(solution)/shard_map/ppermute | solution.py:18
  186.2 7.2 %shard_map.82 = bf16[512,1280]{1,0:T(8,128)(2,1)} custom-call(s32[512,1]{1,0:T(8,128)S(1)} %fusion.41.target_ref, bf16[4,512,1024]{2,1,0:T(8,128)(2,1)} %all-to-all-done.2.late_ref, bf16[4,512,256]{2,1,0:T(8,128)(2,1)S(1)} %all-to-all-done.3.early_ref, f32[512,1280]{1,0:T(8,128)} %fusion.3.derivative_ref), custom_call_target="tpu_custom_call" | custom-call | flops 671088640 | bytes 9175040 | tf_op jit(solution)/shard_map/pallas_call | solution.py:91
  (148 shorter events, 58.1 us)
Async XLA Ops:
  0.7 38.4 %all-to-all-start = ((bf16[32,16,2048]{2,1,0:T(8,128)(2,1)}), bf16[32,16,2048]{2,1,0:T(8,128)(2,1)}, u32[]{:S(2)}, u32[]{:S(2)}) async-start(bf16[32,16,2048]{2,1,0:T(8,128)(2,1)} %bitcast.161), calls=%async_computation | async-start | bytes 4194304 | tf_op jit(solution)/shard_map/all_to_all | solution.py:246
  16.3 16.8 %collective-permute-start.1 = (bf16[2,160,1024]{2,1,0:T(8,128)(2,1)S(1)}, bf16[2,160,1024]{2,1,0:T(8,128)(2,1)S(1)}, u32[]{:S(2)}, u32[]{:S(2)}) collective-permute-start(bf16[2,160,1024]{2,1,0:T(8,128)(2,1)S(1)} %get-tuple-element.33), channel_id=1, source_target_pairs={{0,1},{1,0},{2,3},{3,2},{4,5},{5,4},{6,7},{7,6},{8,9},{9,8},{10,11... | collective-permute-start | bytes 1966088 | tf_op jit(solution)/shard_map/ppermute | solution.py:18
  16.7 17.4 %collective-permute-start.2 = (bf16[2,160,1024]{2,1,0:T(8,128)(2,1)}, bf16[2,160,1024]{2,1,0:T(8,128)(2,1)S(1)}, u32[]{:S(2)}, u32[]{:S(2)}) collective-permute-start(bf16[2,160,1024]{2,1,0:T(8,128)(2,1)} %get-tuple-element.32), channel_id=1, source_target_pairs={{0,3},{1,2},{2,1},{3,0},{4,7},{5,6},{6,5},{7,4},{8,11},{9,10},{10,... | collective-permute-start | bytes 1966088 | tf_op jit(solution)/shard_map/ppermute | solution.py:18
  42.5 38.8 %all-to-all-start.1 = ((bf16[32,16,2048]{2,1,0:T(8,128)(2,1)}), bf16[32,16,2048]{2,1,0:T(8,128)(2,1)S(1)}, u32[]{:S(2)}, u32[]{:S(2)}) async-start(bf16[32,16,2048]{2,1,0:T(8,128)(2,1)} %shard_map.77), calls=%async_computation.1 | async-start | bytes 4194304 | tf_op jit(solution)/shard_map/all_to_all | solution.py:278
  46.5 17.9 %collective-permute-start.5 = (bf16[2,160,1024]{2,1,0:T(8,128)(2,1)}, bf16[2,160,1024]{2,1,0:T(8,128)(2,1)S(1)}, u32[]{:S(2)}, u32[]{:S(2)}) collective-permute-start(bf16[2,160,1024]{2,1,0:T(8,128)(2,1)} %get-tuple-element.32), channel_id=1, source_target_pairs={{0,1},{1,0},{2,3},{3,2},{4,5},{5,4},{6,7},{7,6},{8,9},{9,8},{10,11... | collective-permute-start | bytes 1966088 | tf_op jit(solution)/shard_map/ppermute | solution.py:18
  47.1 18.1 %collective-permute-start.6 = (bf16[2,160,1024]{2,1,0:T(8,128)(2,1)}, bf16[2,160,1024]{2,1,0:T(8,128)(2,1)S(1)}, u32[]{:S(2)}, u32[]{:S(2)}) collective-permute-start(bf16[2,160,1024]{2,1,0:T(8,128)(2,1)} %copy-done.8), channel_id=1, source_target_pairs={{0,3},{1,2},{2,1},{3,0},{4,7},{5,6},{6,5},{7,4},{8,11},{9,10},{10,... | collective-permute-start | bytes 1966088 | tf_op jit(solution)/shard_map/ppermute | solution.py:18
  49.5 29.0 %collective-permute-start.3 = (bf16[2,160,1024]{2,1,0:T(8,128)(2,1)}, bf16[2,160,1024]{2,1,0:T(8,128)(2,1)S(1)}, u32[]{:S(2)}, u32[]{:S(2)}) collective-permute-start(bf16[2,160,1024]{2,1,0:T(8,128)(2,1)} %copy-done.2), channel_id=1, source_target_pairs={{0,3},{1,2},{2,1},{3,0},{4,7},{5,6},{6,5},{7,4},{8,11},{9,10},{10,... | collective-permute-start | bytes 1966088 | tf_op jit(solution)/shard_map/ppermute | solution.py:18
  49.5 29.0 %collective-permute-start.4 = (bf16[2,160,1024]{2,1,0:T(8,128)(2,1)}, bf16[2,160,1024]{2,1,0:T(8,128)(2,1)S(1)}, u32[]{:S(2)}, u32[]{:S(2)}) collective-permute-start(bf16[2,160,1024]{2,1,0:T(8,128)(2,1)} %copy-done.4), channel_id=1, source_target_pairs={{0,1},{1,0},{2,3},{3,2},{4,5},{5,4},{6,7},{7,6},{8,9},{9,8},{10,11... | collective-permute-start | bytes 1966088 | tf_op jit(solution)/shard_map/ppermute | solution.py:18
  92.3 50.6 %collective-permute-start.8 = (bf16[2,4,160,512]{3,2,1,0:T(8,128)(2,1)}, bf16[2,4,160,512]{3,2,1,0:T(8,128)(2,1)}, u32[]{:S(2)}, u32[]{:S(2)}) collective-permute-start(bf16[2,4,160,512]{3,2,1,0:T(8,128)(2,1)} %bitcast.19), channel_id=1, source_target_pairs={{0,8},{8,0},{16,24},{24,16},{1,9},{9,1},{17,25},{25,17},{2,10},{10... | collective-permute-start | bytes 3932168 | tf_op jit(solution)/shard_map/ppermute | solution.py:18
  96.5 48.8 %collective-permute-start.12 = (bf16[2,4,160,512]{3,2,1,0:T(8,128)(2,1)}, bf16[2,4,160,512]{3,2,1,0:T(8,128)(2,1)}, u32[]{:S(2)}, u32[]{:S(2)}) collective-permute-start(bf16[2,4,160,512]{3,2,1,0:T(8,128)(2,1)} %bitcast.21), channel_id=1, source_target_pairs={{0,32},{32,0},{64,96},{96,64},{1,33},{33,1},{65,97},{97,65},{2,34}... | collective-permute-start | bytes 3932168 | tf_op jit(solution)/shard_map/ppermute | solution.py:18
  100.7 47.0 %collective-permute-start.16 = (bf16[2,4,160,512]{3,2,1,0:T(8,128)(2,1)}, bf16[2,4,160,512]{3,2,1,0:T(8,128)(2,1)}, u32[]{:S(2)}, u32[]{:S(2)}) collective-permute-start(bf16[2,4,160,512]{3,2,1,0:T(8,128)(2,1)} %bitcast.23), channel_id=1, source_target_pairs={{0,24},{8,16},{16,8},{24,0},{1,25},{9,17},{17,9},{25,1},{2,26},{10... | collective-permute-start | bytes 3932168 | tf_op jit(solution)/shard_map/ppermute | solution.py:18
  105.4 43.9 %collective-permute-start.20 = (bf16[2,4,160,512]{3,2,1,0:T(8,128)(2,1)}, bf16[2,4,160,512]{3,2,1,0:T(8,128)(2,1)}, u32[]{:S(2)}, u32[]{:S(2)}) collective-permute-start(bf16[2,4,160,512]{3,2,1,0:T(8,128)(2,1)} %bitcast.25), channel_id=1, source_target_pairs={{0,96},{32,64},{64,32},{96,0},{1,97},{33,65},{65,33},{97,1},{2,98}... | collective-permute-start | bytes 3932168 | tf_op jit(solution)/shard_map/ppermute | solution.py:18
  107.5 19.2 %all-to-all-start.3 = ((bf16[4,512,256]{2,1,0:T(8,128)(2,1)}), bf16[4,512,256]{2,1,0:T(8,128)(2,1)S(1)}, u32[]{:S(2)}, u32[]{:S(2)}) async-start(bf16[4,512,256]{2,1,0:T(8,128)(2,1)} %shard_map.81), calls=%async_computation.3 | async-start | bytes 2097152 | tf_op jit(solution)/shard_map/all_to_all | solution.py:284
  126.7 59.5 %all-to-all-start.2 = ((bf16[4,512,1024]{2,1,0:T(8,128)(2,1)}), bf16[4,512,1024]{2,1,0:T(8,128)(2,1)}, u32[]{:S(2)}, u32[]{:S(2)}) async-start(bf16[4,512,1024]{2,1,0:T(8,128)(2,1)} %shard_map.80), calls=%async_computation.2 | async-start | bytes 8388608 | tf_op jit(solution)/shard_map/all_to_all | solution.py:284
  144.1 16.1 %collective-permute-start.9 = (bf16[4,160,512]{2,1,0:T(8,128)(2,1)S(1)}, bf16[4,160,512]{2,1,0:T(8,128)(2,1)S(1)}, u32[]{:S(2)}, u32[]{:S(2)}) collective-permute-start(bf16[4,160,512]{2,1,0:T(8,128)(2,1)S(1)} %fusion.26), channel_id=1, source_target_pairs={{0,24},{8,16},{16,8},{24,0},{1,25},{9,17},{17,9},{25,1},{2,26},{10... | collective-permute-start | bytes 1966088 | tf_op jit(solution)/shard_map/ppermute | solution.py:18
  146.6 15.8 %collective-permute-start.13 = (bf16[4,160,512]{2,1,0:T(8,128)(2,1)S(1)}, bf16[4,160,512]{2,1,0:T(8,128)(2,1)S(1)}, u32[]{:S(2)}, u32[]{:S(2)}) collective-permute-start(bf16[4,160,512]{2,1,0:T(8,128)(2,1)S(1)} %fusion.23), channel_id=1, source_target_pairs={{0,96},{32,64},{64,32},{96,0},{1,97},{33,65},{65,33},{97,1},{2,98}... | collective-permute-start | bytes 1966088 | tf_op jit(solution)/shard_map/ppermute | solution.py:18
  149.0 15.0 %collective-permute-start.17 = (bf16[4,160,512]{2,1,0:T(8,128)(2,1)S(1)}, bf16[4,160,512]{2,1,0:T(8,128)(2,1)S(1)}, u32[]{:S(2)}, u32[]{:S(2)}) collective-permute-start(bf16[4,160,512]{2,1,0:T(8,128)(2,1)S(1)} %fusion.20), channel_id=1, source_target_pairs={{0,8},{8,0},{16,24},{24,16},{1,9},{9,1},{17,25},{25,17},{2,10},{10... | collective-permute-start | bytes 1966088 | tf_op jit(solution)/shard_map/ppermute | solution.py:18
  150.6 17.7 %collective-permute-start.21 = (bf16[4,160,512]{2,1,0:T(8,128)(2,1)S(1)}, bf16[4,160,512]{2,1,0:T(8,128)(2,1)S(1)}, u32[]{:S(2)}, u32[]{:S(2)}) collective-permute-start(bf16[4,160,512]{2,1,0:T(8,128)(2,1)S(1)} %fusion.17), channel_id=1, source_target_pairs={{0,32},{32,0},{64,96},{96,64},{1,33},{33,1},{65,97},{97,65},{2,34}... | collective-permute-start | bytes 1966088 | tf_op jit(solution)/shard_map/ppermute | solution.py:18
  161.6 10.6 %collective-permute-start.10 = (bf16[2,160,512]{2,1,0:T(8,128)(2,1)S(1)}, bf16[2,160,512]{2,1,0:T(8,128)(2,1)S(1)}, u32[]{:S(2)}, u32[]{:S(2)}) collective-permute-start(bf16[2,160,512]{2,1,0:T(8,128)(2,1)S(1)} %slice.239), channel_id=1, source_target_pairs={{0,32},{32,0},{64,96},{96,64},{1,33},{33,1},{65,97},{97,65},{2,34}... | collective-permute-start | bytes 983048 | tf_op jit(solution)/shard_map/ppermute | solution.py:18
  163.8 10.5 %collective-permute-start.14 = (bf16[2,160,512]{2,1,0:T(8,128)(2,1)S(1)}, bf16[2,160,512]{2,1,0:T(8,128)(2,1)S(1)}, u32[]{:S(2)}, u32[]{:S(2)}) collective-permute-start(bf16[2,160,512]{2,1,0:T(8,128)(2,1)S(1)} %slice.248), channel_id=1, source_target_pairs={{0,8},{8,0},{16,24},{24,16},{1,9},{9,1},{17,25},{25,17},{2,10},{10... | collective-permute-start | bytes 983048 | tf_op jit(solution)/shard_map/ppermute | solution.py:18
  165.3 11.2 %collective-permute-start.18 = (bf16[2,160,512]{2,1,0:T(8,128)(2,1)S(1)}, bf16[2,160,512]{2,1,0:T(8,128)(2,1)S(1)}, u32[]{:S(2)}, u32[]{:S(2)}) collective-permute-start(bf16[2,160,512]{2,1,0:T(8,128)(2,1)S(1)} %slice.257), channel_id=1, source_target_pairs={{0,96},{32,64},{64,32},{96,0},{1,97},{33,65},{65,33},{97,1},{2,98}... | collective-permute-start | bytes 983048 | tf_op jit(solution)/shard_map/ppermute | solution.py:18
  169.6 10.1 %collective-permute-start.22 = (bf16[2,160,512]{2,1,0:T(8,128)(2,1)S(1)}, bf16[2,160,512]{2,1,0:T(8,128)(2,1)S(1)}, u32[]{:S(2)}, u32[]{:S(2)}) collective-permute-start(bf16[2,160,512]{2,1,0:T(8,128)(2,1)S(1)} %slice.266), channel_id=1, source_target_pairs={{0,24},{8,16},{16,8},{24,0},{1,25},{9,17},{17,9},{25,1},{2,26},{10... | collective-permute-start | bytes 983048 | tf_op jit(solution)/shard_map/ppermute | solution.py:18
  172.2 8.1 %collective-permute-start.11 = (bf16[160,512]{1,0:T(8,128)(2,1)S(1)}, bf16[160,512]{1,0:T(8,128)(2,1)S(1)}, u32[]{:S(2)}, u32[]{:S(2)}) collective-permute-start(bf16[160,512]{1,0:T(8,128)(2,1)S(1)} %fusion.47), channel_id=1, source_target_pairs={{0,96},{32,64},{64,32},{96,0},{1,97},{33,65},{65,33},{97,1},{2,98}... | collective-permute-start | bytes 491528 | tf_op jit(solution)/shard_map/ppermute | solution.py:18
  174.3 7.2 %collective-permute-start.15 = (bf16[160,512]{1,0:T(8,128)(2,1)S(1)}, bf16[160,512]{1,0:T(8,128)(2,1)S(1)}, u32[]{:S(2)}, u32[]{:S(2)}) collective-permute-start(bf16[160,512]{1,0:T(8,128)(2,1)S(1)} %fusion.48), channel_id=1, source_target_pairs={{0,24},{8,16},{16,8},{24,0},{1,25},{9,17},{17,9},{25,1},{2,26},{10... | collective-permute-start | bytes 491528 | tf_op jit(solution)/shard_map/ppermute | solution.py:18
  (30 other events, 227.4 us)
